TPU v7x, 32 devices: a whole 2x2x4 slice. The times are simulated.
32 devices in a mesh: wide: 4 (over y, core), narrow: 8 (over z, x).
Axes of the slice: x: 2, y: 2, z: 4, core: 2. Of those that a mesh axis runs over, the one named last changes fastest.
Arguments:
- transmission: float32 [2, 4096, 2048], P(None, 'narrow', 'wide'), may hold values from -5 to 5
- probe_wave: float32 [2, 256, 256], replicated, may hold values from -5 to 5
- positions: int32 [8, 4, 2, 6, 2], P('narrow', 'wide'), may hold values from 0 to 512, as said below
- counts: int32 [8, 4, 2], P('narrow', 'wide'), may hold values from 1 to 6, as said below
- measured: float32 [8, 4, 2, 6, 256, 256], P('narrow', 'wide'), may hold values from 0 to 2
Outputs:
- updated: float32 [2, 4096, 2048], P(None, 'narrow', 'wide')
Inputs may be any that keep to these rules, and one draw needn't show every extreme that they name: `positions`: offsets in pixels from the upper left corner of the tile's reach, which begins 128 pixels before the tile; both ends are taken in every draw. `counts`: some tile and subset has all 6 slots live in every draw; loads differ from tile to tile.
All inputs are finite; a program needn't handle non-finite values.
Results may differ from a plain program's by a relative error of at most 0.0001.
Values sent between devices are 32-bit elements; how exact they have to be, the bound alone decides.
No kernel may reach another device: no remote copies, remote signals or barrier semaphores. Data moves between devices by JAX's collectives and lax.ppermute only.
A program may use at most 128 MiB of HBM per device.

v0:
```python
import math

import jax
import jax.numpy as jnp
from jax import lax
from jax.sharding import PartitionSpec as P

HALO = 128


FLOOR_VALUE = 0.5


def shifted(shard, axis, by):
    count = lax.axis_size(axis)
    pairs = [(i, i + by) for i in range(count) if 0 <= i + by < count]
    return lax.ppermute(shard, axis, pairs)


def with_halo(shard, sides, width):
    for axis, dim in sides:
        count, length = (lax.axis_size(axis), shard.shape[dim])
        up = [(i, (i + 1) % count) for i in range(count - 1)]
        down = [(j, i) for i, j in up]
        last = lax.slice_in_dim(shard, length - width, length, axis=dim)
        leading = lax.slice_in_dim(shard, 0, width, axis=dim)
        before = lax.ppermute(last, axis, up)
        after = lax.ppermute(leading, axis, down)
        shard = jnp.concatenate([before, shard, after], axis=dim)
    return shard


def tables(window):
    steps_along = jnp.arange(window, dtype=jnp.int32)
    product = steps_along[:, None] * steps_along[None, :] % window
    phases = product.astype(jnp.float32) * (2.0 * math.pi / window)
    factor = 1.0 / math.sqrt(window)
    return (jnp.cos(phases) * factor, jnp.sin(phases) * factor)


def left_multiply(matrix_re, matrix_im, data_re, data_im):
    first_term = jnp.einsum("jk,bkl->bjl", matrix_re, data_re, precision=lax.Precision.HIGHEST)
    second_term = jnp.einsum("jk,bkl->bjl", matrix_im, data_im, precision=lax.Precision.HIGHEST)
    third_term = jnp.einsum("jk,bkl->bjl", matrix_re, data_im, precision=lax.Precision.HIGHEST)
    fourth_term = jnp.einsum("jk,bkl->bjl", matrix_im, data_re, precision=lax.Precision.HIGHEST)
    return (first_term - second_term, third_term + fourth_term)


def right_multiply(data_re, data_im, matrix_re, matrix_im):
    first_term = jnp.einsum("bjk,kl->bjl", data_re, matrix_re, precision=lax.Precision.HIGHEST)
    second_term = jnp.einsum("bjk,kl->bjl", data_im, matrix_im, precision=lax.Precision.HIGHEST)
    third_term = jnp.einsum("bjk,kl->bjl", data_im, matrix_re, precision=lax.Precision.HIGHEST)
    fourth_term = jnp.einsum("bjk,kl->bjl", data_re, matrix_im, precision=lax.Precision.HIGHEST)
    return (first_term - second_term, third_term + fourth_term)


def subset_gradient(
    extended, probe_re, probe_im, cosine_table, sine_table, starts, amplitudes, live_count
):
    window = probe_re.shape[0]
    slot_number = starts.shape[0]

    def cut_window(start_pair):
        zero_start = jnp.zeros((), jnp.int32)
        return lax.dynamic_slice(
            extended, (zero_start, start_pair[0], start_pair[1]), (2, window, window)
        )

    windows = jax.vmap(cut_window)(starts)
    wave_re = probe_re[None] * windows[:, 0] - probe_im[None] * windows[:, 1]
    wave_im = probe_re[None] * windows[:, 1] + probe_im[None] * windows[:, 0]
    spec_re, spec_im = left_multiply(cosine_table, -sine_table, wave_re, wave_im)
    spec_re, spec_im = right_multiply(spec_re, spec_im, cosine_table, -sine_table)
    magnitude = jnp.maximum(jnp.sqrt(spec_re * spec_re + spec_im * spec_im), FLOOR_VALUE)
    ratio = amplitudes / magnitude
    proj_re = spec_re * ratio
    proj_im = spec_im * ratio
    back_re, back_im = left_multiply(cosine_table, sine_table, proj_re, proj_im)
    back_re, back_im = right_multiply(back_re, back_im, cosine_table, sine_table)
    diff_re = back_re - wave_re
    diff_im = back_im - wave_im
    grad_re = probe_re[None] * diff_re + probe_im[None] * diff_im
    grad_im = probe_re[None] * diff_im - probe_im[None] * diff_re
    live_mask = (jnp.arange(slot_number, dtype=jnp.int32) < live_count)[:, None, None]
    grad_re = jnp.where(live_mask, grad_re, 0.0)
    grad_im = jnp.where(live_mask, grad_im, 0.0)
    gradient = jnp.zeros_like(extended)
    zero_start = jnp.zeros((), jnp.int32)
    for slot_index in range(slot_number):
        place = (zero_start, starts[slot_index, 0], starts[slot_index, 1])
        current = lax.dynamic_slice(gradient, place, (2, window, window))
        addition = jnp.stack([grad_re[slot_index], grad_im[slot_index]])
        gradient = lax.dynamic_update_slice(gradient, current + addition, place)
    return gradient


def fold_rims(gradient):
    upper_rows = gradient[:, :HALO, :]
    lower_rows = gradient[:, -HALO:, :]
    middle = gradient[:, HALO:-HALO, :]
    from_above = shifted(lower_rows, "narrow", 1)
    from_below = shifted(upper_rows, "narrow", -1)
    middle = middle.at[:, :HALO, :].add(from_above)
    middle = middle.at[:, -HALO:, :].add(from_below)
    left_cols = middle[:, :, :HALO]
    right_cols = middle[:, :, -HALO:]
    center = middle[:, :, HALO:-HALO]
    from_left = shifted(right_cols, "wide", 1)
    from_right = shifted(left_cols, "wide", -1)
    center = center.at[:, :, :HALO].add(from_left)
    center = center.at[:, :, -HALO:].add(from_right)
    return center


def shards(transmission, probe_wave, positions, counts, measured):
    row_extended = with_halo(transmission, (("narrow", 1),), HALO)
    extended = with_halo(row_extended, (("wide", 2),), HALO)
    probe_re = probe_wave[0]
    probe_im = probe_wave[1]
    step_scale = 1.0 / jnp.max(probe_re * probe_re + probe_im * probe_im)
    cosine_table, sine_table = tables(probe_re.shape[0])
    gradient_one = subset_gradient(
        extended,
        probe_re,
        probe_im,
        cosine_table,
        sine_table,
        positions[0, 0, 0],
        measured[0, 0, 0],
        counts[0, 0, 0],
    )
    gradient_two = subset_gradient(
        extended,
        probe_re,
        probe_im,
        cosine_table,
        sine_table,
        positions[0, 0, 1],
        measured[0, 0, 1],
        counts[0, 0, 1],
    )
    update = fold_rims(gradient_one + gradient_two)
    return transmission + step_scale * update


def solution(mesh):
    in_specs = (
        P(None, "narrow", "wide"),
        P(),
        P("narrow", "wide", None, None, None),
        P("narrow", "wide", None),
        P("narrow", "wide", None, None, None, None),
    )
    out_specs = P(None, "narrow", "wide")
    return jax.shard_map(shards, mesh=mesh, in_specs=in_specs, out_specs=out_specs, check_vma=False)
```

profile of v0, /device:TPU:25, one launch (start us, length us, event | category | flops | bytes accessed | tf_op | source)
XLA Modules:
  0.0 406.5 jit_solution(11667983707267910576)
XLA Ops:
  55.5 4.4 %collective-permute-start.2 = (f32[2,768,128]{2,1,0:T(8,128)S(1)}, f32[2,768,128]{2,1,0:T(8,128)S(1)}, u32[]{:S(2)}, u32[]{:S(2)}) collective-permute-start(f32[2,768,128]{2,1,0:T(8,128)S(1)} %get-tuple-element.107), channel_id=1, source_target_pairs={{0,8},{8,16},{16,24},{1,9},{9,17},{17,25},{2,10},{10,18},{18,26},{... | collective-permute-start | bytes 2359304 | tf_op jit(solution)/shard_map/ppermute | solution.py:27
  64.4 4.4 %collective-permute-done.2 = f32[2,768,128]{2,1,0:T(8,128)S(1)} collective-permute-done((f32[2,768,128]{2,1,0:T(8,128)S(1)}, f32[2,768,128]{2,1,0:T(8,128)S(1)}, u32[]{:S(2)}, u32[]{:S(2)}) %collective-permute-start.2) | collective-permute-done | bytes 786464 | tf_op jit(solution)/shard_map/ppermute | solution.py:27
  68.8 4.4 %collective-permute-done.3 = f32[2,768,128]{2,1,0:T(8,128)S(1)} collective-permute-done((f32[2,768,128]{2,1,0:T(8,128)S(1)}, f32[2,768,128]{2,1,0:T(8,128)S(1)}, u32[]{:S(2)}, u32[]{:S(2)}) %collective-permute-start.3) | collective-permute-done | bytes 786464 | tf_op jit(solution)/shard_map/ppermute | solution.py:28
  76.0 19.7 %while.6 = (s32[]{:T(128)}, f32[2,768,768]{2,1,0:T(8,128)}, s32[6,3]{0,1:T(4,128)S(1)}, f32[6,2,256,256]{3,2,0,1:T(8,128)S(1)}, s32[]{:T(128)}) while((s32[]{:T(128)}, f32[2,768,768]{2,1,0:T(8,128)}, s32[6,3]{0,1:T(4,128)S(1)}, f32[6,2,256,256]{3,2,0,1:T(8,128)S(1)}, s32[]{:T(128)}) %tuple.119), condition=%wide.while_cond.4, body=%wide.while_body.4.sunk | while | flops 2 | bytes 1048693 | solution.py:65
  97.7 25.3 %while.7 = (s32[]{:T(128)}, f32[2,768,768]{2,1,0:T(8,128)}, s32[6,3]{0,1:T(4,128)S(1)}, f32[6,2,256,256]{3,2,0,1:T(8,128)}, s32[]{:T(128)}) while((s32[]{:T(128)}, f32[2,768,768]{2,1,0:T(8,128)}, s32[6,3]{0,1:T(4,128)S(1)}, f32[6,2,256,256]{3,2,0,1:T(8,128)}, s32[]{:T(128)}) %tuple.122), condition=%wide.while_cond.5, body=%wide.while_body.5.sunk | while | flops 2 | bytes 1050217 | solution.py:65
  158.8 4.1 %fusion.10 = f32[6,256,256]{2,1,0:T(8,128)S(1)} fusion(f32[6,256,256]{2,1,0:T(8,128)S(1)} %convolution_add_fusion.1), kind=kOutput, calls=%fused_computation.17 | convolution fusion | flops 1209008128 | bytes 3145728 | tf_op jit(solution)/shard_map/bjk,kl->bjl/dot_general | solution.py:51
  181.3 4.9 %fusion.37 = (f32[6,256,256]{2,1,0:T(8,128)S(1)}, f32[6,256,256]{2,1,0:T(8,128)S(1)}, f32[6,256,256]{2,1,0:T(8,128)S(1)}, f32[6,256,256]{2,1,0:T(8,128)S(1)}) fusion(f32[6,256,256]{2,1,0:T(8,128)S(1)} %fusion.53, f32[1,1,2,6,256,256]{5,4,3,2,1,0:T(8,128)S(1)} %copy-done.11, f32[6,256,256]{2,1,0:T(8,128)S(1)} %fusion.43, f32[6,256,256]{2,1,0:T(8,128)S(1)} %fusion.40, ...), kind=kOutput, calls=%fused_computation.57 | convolution fusion | flops 1214840832 | bytes 17301504 | tf_op jit(solution)/shard_map/bjk,kl->bjl/dot_general | solution.py:50
  197.0 4.0 fusion.18
  241.4 4.9 %add_select_fusion = (f32[6,256,256]{2,1,0:T(8,128)S(1)}, f32[6,256,256]{2,1,0:T(8,128)S(1)}, f32[6,256,256]{2,1,0:T(8,128)S(1)}, f32[6,256,256]{2,1,0:T(8,128)S(1)}) fusion(f32[6,256,256]{2,1,0:T(8,128)S(1)} %subtract_subtract_fusion, f32[256,256]{1,0:T(8,128)S(1)} %copy-done.2, f32[256,256]{1,0:T(8,128)S(1)} %get-tuple-element.139, ...), kind=kOutput, calls=%fused_computation.53 | convolution fusion | flops 1216020480 | bytes 16252940 | tf_op jit(solution)/shard_map/bjk,kl->bjl/dot_general | solution.py:53
  251.7 6.8 %dynamic_update_slice.42 = f32[2,768,768]{2,1,0:T(8,128)} dynamic-update-slice(f32[2,768,768]{2,1,0:T(8,128)} %broadcast.108.clone.1, f32[2,256,256]{2,1,0:T(8,128)} %pad_maximum_fusion.2, s32[]{:T(128)} %constant.131.clone.1, s32[]{:T(128)S(6)} %select_n.211, s32[]{:T(128)S(6)} %select_n.212) | dynamic-update-slice | bytes 1048580 | tf_op jit(solution)/shard_map/dynamic_update_slice | solution.py:93
  260.8 6.4 %dynamic_update_slice.43 = f32[2,768,768]{2,1,0:T(8,128)} dynamic-update-slice(f32[2,768,768]{2,1,0:T(8,128)} %dynamic_update_slice.42, f32[2,256,256]{2,1,0:T(8,128)} %maximum_add_fusion.5, s32[]{:T(128)} %constant.131.clone.1, s32[]{:T(128)S(6)} %select_n.213, s32[]{:T(128)S(6)} %select_n.214) | dynamic-update-slice | bytes 1048580 | tf_op jit(solution)/shard_map/dynamic_update_slice | solution.py:93
  269.5 6.8 %dynamic_update_slice.44 = f32[2,768,768]{2,1,0:T(8,128)} dynamic-update-slice(f32[2,768,768]{2,1,0:T(8,128)} %dynamic_update_slice.43, f32[2,256,256]{2,1,0:T(8,128)} %maximum_add_fusion.6, s32[]{:T(128)} %constant.131.clone.1, s32[]{:T(128)S(6)} %select_n.215, s32[]{:T(128)S(6)} %select_n.216) | dynamic-update-slice | bytes 1048580 | tf_op jit(solution)/shard_map/dynamic_update_slice | solution.py:93
  278.7 6.5 %dynamic_update_slice.45 = f32[2,768,768]{2,1,0:T(8,128)} dynamic-update-slice(f32[2,768,768]{2,1,0:T(8,128)} %dynamic_update_slice.44, f32[2,256,256]{2,1,0:T(8,128)} %maximum_add_fusion.7, s32[]{:T(128)} %constant.131.clone.1, s32[]{:T(128)S(6)} %select_n.217, s32[]{:T(128)S(6)} %select_n.218) | dynamic-update-slice | bytes 1048580 | tf_op jit(solution)/shard_map/dynamic_update_slice | solution.py:93
  287.5 6.7 %dynamic_update_slice.46 = f32[2,768,768]{2,1,0:T(8,128)} dynamic-update-slice(f32[2,768,768]{2,1,0:T(8,128)} %dynamic_update_slice.45, f32[2,256,256]{2,1,0:T(8,128)} %maximum_add_fusion.8, s32[]{:T(128)} %constant.131.clone.1, s32[]{:T(128)S(6)} %select_n.219, s32[]{:T(128)S(6)} %select_n.220) | dynamic-update-slice | bytes 1048580 | tf_op jit(solution)/shard_map/dynamic_update_slice | solution.py:93
  296.5 6.8 %dynamic_update_slice.47 = f32[2,768,768]{2,1,0:T(8,128)} dynamic-update-slice(f32[2,768,768]{2,1,0:T(8,128)} %dynamic_update_slice.46, f32[2,256,256]{2,1,0:T(8,128)} %maximum_add_fusion.9, s32[]{:T(128)} %constant.131.clone.1, s32[]{:T(128)S(6)} %select_n.221, s32[]{:T(128)S(6)} %select_n.222) | dynamic-update-slice | bytes 1048580 | tf_op jit(solution)/shard_map/dynamic_update_slice | solution.py:93
  307.0 6.0 %dynamic_update_slice.36 = f32[2,768,768]{2,1,0:T(8,128)} dynamic-update-slice(f32[2,768,768]{2,1,0:T(8,128)} %broadcast.108.clone, f32[2,256,256]{2,1,0:T(8,128)S(1)} %pad_maximum_fusion.1, s32[]{:T(128)} %constant.131.clone.1, s32[]{:T(128)S(6)} %select_n.195, s32[]{:T(128)S(6)} %select_n.196) | dynamic-update-slice | bytes 1048580 | tf_op jit(solution)/shard_map/dynamic_update_slice | solution.py:93
  314.4 6.1 %dynamic_update_slice.37 = f32[2,768,768]{2,1,0:T(8,128)} dynamic-update-slice(f32[2,768,768]{2,1,0:T(8,128)} %dynamic_update_slice.36, f32[2,256,256]{2,1,0:T(8,128)S(1)} %maximum_add_fusion, s32[]{:T(128)} %constant.131.clone.1, s32[]{:T(128)S(6)} %select_n.197, s32[]{:T(128)S(6)} %select_n.198) | dynamic-update-slice | bytes 1048580 | tf_op jit(solution)/shard_map/dynamic_update_slice | solution.py:93
  321.9 6.5 %dynamic_update_slice.38 = f32[2,768,768]{2,1,0:T(8,128)} dynamic-update-slice(f32[2,768,768]{2,1,0:T(8,128)} %dynamic_update_slice.37, f32[2,256,256]{2,1,0:T(8,128)S(1)} %maximum_add_fusion.1, s32[]{:T(128)} %constant.131.clone.1, s32[]{:T(128)S(6)} %select_n.199, s32[]{:T(128)S(6)} %select_n.200) | dynamic-update-slice | bytes 1048580 | tf_op jit(solution)/shard_map/dynamic_update_slice | solution.py:93
  329.9 6.4 %dynamic_update_slice.39 = f32[2,768,768]{2,1,0:T(8,128)} dynamic-update-slice(f32[2,768,768]{2,1,0:T(8,128)} %dynamic_update_slice.38, f32[2,256,256]{2,1,0:T(8,128)S(1)} %maximum_add_fusion.2, s32[]{:T(128)} %constant.131.clone.1, s32[]{:T(128)S(6)} %select_n.201, s32[]{:T(128)S(6)} %select_n.202) | dynamic-update-slice | bytes 1048580 | tf_op jit(solution)/shard_map/dynamic_update_slice | solution.py:93
  337.7 6.7 %dynamic_update_slice.40 = f32[2,768,768]{2,1,0:T(8,128)} dynamic-update-slice(f32[2,768,768]{2,1,0:T(8,128)} %dynamic_update_slice.39, f32[2,256,256]{2,1,0:T(8,128)S(1)} %maximum_add_fusion.3, s32[]{:T(128)} %constant.131.clone.1, s32[]{:T(128)S(6)} %select_n.203, s32[]{:T(128)S(6)} %select_n.204) | dynamic-update-slice | bytes 1048580 | tf_op jit(solution)/shard_map/dynamic_update_slice | solution.py:93
  345.7 6.8 %dynamic_update_slice.41 = f32[2,768,768]{2,1,0:T(8,128)} dynamic-update-slice(f32[2,768,768]{2,1,0:T(8,128)} %dynamic_update_slice.40, f32[2,256,256]{2,1,0:T(8,128)S(1)} %maximum_add_fusion.4, s32[]{:T(128)} %constant.131.clone.1, s32[]{:T(128)S(6)} %select_n.205, s32[]{:T(128)S(6)} %select_n.206) | dynamic-update-slice | bytes 1048580 | tf_op jit(solution)/shard_map/dynamic_update_slice | solution.py:93
  352.5 4.4 %add.355 = f32[2,768,768]{2,1,0:T(8,128)S(1)} add(f32[2,768,768]{2,1,0:T(8,128)} %dynamic_update_slice.41, f32[2,768,768]{2,1,0:T(8,128)} %dynamic_update_slice.47) | non-fusion elementwise | flops 1179648 | bytes 14155776 | tf_op jit(solution)/shard_map/add | solution.py:142
  363.4 9.0 %collective-permute-done.4 = f32[2,128,768]{2,1,0:T(8,128)S(1)} collective-permute-done((f32[2,128,768]{2,1,0:T(8,128)S(1)}, f32[2,128,768]{2,1,0:T(8,128)S(1)}, u32[]{:S(2)}, u32[]{:S(2)}) %collective-permute-start.4) | collective-permute-done | bytes 786464 | tf_op jit(solution)/shard_map/ppermute | solution.py:17
  372.5 16.8 %collective-permute-done.5 = f32[2,128,768]{2,1,0:T(8,128)S(1)} collective-permute-done((f32[2,128,768]{2,1,0:T(8,128)S(1)}, f32[2,128,768]{2,1,0:T(8,128)S(1)}, u32[]{:S(2)}, u32[]{:S(2)}) %collective-permute-start.5) | collective-permute-done | bytes 786464 | tf_op jit(solution)/shard_map/ppermute | solution.py:17
  (145 shorter events, 219.5 us)
Async XLA Ops:
  0.0 55.1 %copy-start = (f32[2,512,512]{2,1,0:T(8,128)S(1)}, f32[2,512,512]{2,1,0:T(8,128)}, u32[]{:S(2)}) copy-start(f32[2,512,512]{2,1,0:T(8,128)} %param.13) | copy-start | bytes 6291460
  0.0 8.6 %copy-start.9 = (s32[1,1,2,6,2]{3,4,2,1,0:T(2,128)S(1)}, s32[1,1,2,6,2]{3,4,2,1,0:T(2,128)}, u32[]{:S(2)}) copy-start(s32[1,1,2,6,2]{3,4,2,1,0:T(2,128)} %param.15) | copy-start | bytes 292
  2.4 52.6 %collective-permute-start = (f32[2,128,512]{2,1,0:T(8,128)}, f32[2,128,512]{2,1,0:T(8,128)S(1)}, u32[]{:S(2)}, u32[]{:S(2)}) collective-permute-start(f32[2,128,512]{2,1,0:T(8,128)} %get-tuple-element.110), channel_id=1, source_target_pairs={{0,1},{1,2},{2,3},{3,4},{4,5},{5,6},{6,7},{8,9},{9,10},{10,11},{11... | collective-permute-start | bytes 1572872 | tf_op jit(solution)/shard_map/ppermute | solution.py:27
  5.5 49.8 %collective-permute-start.1 = (f32[2,128,512]{2,1,0:T(8,128)}, f32[2,128,512]{2,1,0:T(8,128)S(1)}, u32[]{:S(2)}, u32[]{:S(2)}) collective-permute-start(f32[2,128,512]{2,1,0:T(8,128)} %get-tuple-element.109), channel_id=1, source_target_pairs={{1,0},{2,1},{3,2},{4,3},{5,4},{6,5},{7,6},{9,8},{10,9},{11,10},{12... | collective-permute-start | bytes 1572872 | tf_op jit(solution)/shard_map/ppermute | solution.py:28
  55.3 6.5 %copy-start.10 = (s32[1,1,2]{2,1,0:T(1,128)S(1)}, s32[1,1,2]{2,1,0:T(1,128)}, u32[]{:S(2)}) copy-start(s32[1,1,2]{2,1,0:T(1,128)} %param.16) | copy-start | bytes 28
  55.4 8.3 %copy-start.3 = (f32[2,256,256]{2,1,0:T(8,128)S(1)}, f32[2,256,256]{2,1,0:T(8,128)}, u32[]{:S(2)}) copy-start(f32[2,256,256]{2,1,0:T(8,128)} %param.14) | copy-start | bytes 1572868
  55.5 13.3 %collective-permute-start.2 = (f32[2,768,128]{2,1,0:T(8,128)S(1)}, f32[2,768,128]{2,1,0:T(8,128)S(1)}, u32[]{:S(2)}, u32[]{:S(2)}) collective-permute-start(f32[2,768,128]{2,1,0:T(8,128)S(1)} %get-tuple-element.107), channel_id=1, source_target_pairs={{0,8},{8,16},{16,24},{1,9},{9,17},{17,25},{2,10},{10,18},{18,26},{... | collective-permute-start | bytes 2359304 | tf_op jit(solution)/shard_map/ppermute | solution.py:27
  59.9 13.3 %collective-permute-start.3 = (f32[2,768,128]{2,1,0:T(8,128)S(1)}, f32[2,768,128]{2,1,0:T(8,128)S(1)}, u32[]{:S(2)}, u32[]{:S(2)}) collective-permute-start(f32[2,768,128]{2,1,0:T(8,128)S(1)} %get-tuple-element.108), channel_id=1, source_target_pairs={{8,0},{16,8},{24,16},{9,1},{17,9},{25,17},{10,2},{18,10},{26,18},{... | collective-permute-start | bytes 2359304 | tf_op jit(solution)/shard_map/ppermute | solution.py:28
  177.7 3.6 copy-start.11
  237.8 3.6 copy-start.2
  304.5 8.5 %copy-start.8 = (f32[1,256,256]{2,1,0:T(8,128)S(1)}, f32[1,256,256]{2,1,0:T(8,128)}, u32[]{:S(2)}) copy-start(f32[1,256,256]{2,1,0:T(8,128)} %get-tuple-element.127) | copy-start | bytes 786436
  313.0 7.5 %copy-start.7 = (f32[1,256,256]{2,1,0:T(8,128)S(1)}, f32[1,256,256]{2,1,0:T(8,128)}, u32[]{:S(2)}) copy-start(f32[1,256,256]{2,1,0:T(8,128)} %get-tuple-element.126) | copy-start | bytes 786436
  320.5 7.9 %copy-start.6 = (f32[1,256,256]{2,1,0:T(8,128)S(1)}, f32[1,256,256]{2,1,0:T(8,128)}, u32[]{:S(2)}) copy-start(f32[1,256,256]{2,1,0:T(8,128)} %get-tuple-element.125) | copy-start | bytes 786436
  328.5 7.9 %copy-start.5 = (f32[1,256,256]{2,1,0:T(8,128)S(1)}, f32[1,256,256]{2,1,0:T(8,128)}, u32[]{:S(2)}) copy-start(f32[1,256,256]{2,1,0:T(8,128)} %get-tuple-element.124) | copy-start | bytes 786436
  357.0 15.4 %collective-permute-start.4 = (f32[2,128,768]{2,1,0:T(8,128)S(1)}, f32[2,128,768]{2,1,0:T(8,128)S(1)}, u32[]{:S(2)}, u32[]{:S(2)}) collective-permute-start(f32[2,128,768]{2,1,0:T(8,128)S(1)} %get-tuple-element.94), channel_id=1, source_target_pairs={{0,1},{1,2},{2,3},{3,4},{4,5},{5,6},{6,7},{8,9},{9,10},{10,11},{11... | collective-permute-start | bytes 2359304 | tf_op jit(solution)/shard_map/ppermute | solution.py:17
  360.9 28.4 %collective-permute-start.5 = (f32[2,128,768]{2,1,0:T(8,128)S(1)}, f32[2,128,768]{2,1,0:T(8,128)S(1)}, u32[]{:S(2)}, u32[]{:S(2)}) collective-permute-start(f32[2,128,768]{2,1,0:T(8,128)S(1)} %get-tuple-element.93), channel_id=1, source_target_pairs={{1,0},{2,1},{3,2},{4,3},{5,4},{6,5},{7,6},{9,8},{10,9},{11,10},{12... | collective-permute-start | bytes 2359304 | tf_op jit(solution)/shard_map/ppermute | solution.py:17
  389.5 6.2 %copy-start.4 = (f32[2,256,256]{2,1,0:T(8,128)S(1)}, f32[2,256,256]{2,1,0:T(8,128)}, u32[]{:S(2)}) copy-start(f32[2,256,256]{2,1,0:T(8,128)} %param.14) | copy-start | bytes 1572868
  390.6 8.3 %collective-permute-start.6 = (f32[2,512,128]{2,1,0:T(8,128)}, f32[2,512,128]{2,1,0:T(8,128)}, u32[]{:S(2)}, u32[]{:S(2)}) collective-permute-start(f32[2,512,128]{2,1,0:T(8,128)} %get-tuple-element.104), channel_id=1, source_target_pairs={{0,8},{8,16},{16,24},{1,9},{9,17},{17,25},{2,10},{10,18},{18,26},{... | collective-permute-start | bytes 1572872 | tf_op jit(solution)/shard_map/ppermute | solution.py:17
  392.5 10.8 %collective-permute-start.7 = (f32[2,512,128]{2,1,0:T(8,128)}, f32[2,512,128]{2,1,0:T(8,128)}, u32[]{:S(2)}, u32[]{:S(2)}) collective-permute-start(f32[2,512,128]{2,1,0:T(8,128)} %get-tuple-element.103), channel_id=1, source_target_pairs={{8,0},{16,8},{24,16},{9,1},{17,9},{25,17},{10,2},{18,10},{26,18},{... | collective-permute-start | bytes 1572872 | tf_op jit(solution)/shard_map/ppermute | solution.py:17
  397.4 7.1 %copy-start.1 = (f32[2,512,512]{2,1,0:T(8,128)S(1)}, f32[2,512,512]{2,1,0:T(8,128)}, u32[]{:S(2)}) copy-start(f32[2,512,512]{2,1,0:T(8,128)} %param.13) | copy-start | bytes 6291460
where the time goes:
time: 413 us; the launch traced here: 406 us
  local copies, waits for them, and re-layouts  141 us (34%)
  matrix products  120 us (29%)
  between operations  46.6 us (11%)
  waiting for transfers between devices  39.4 us (10%)
  other arithmetic  35.3 us (9%)
  starting transfers between devices  23.8 us (6%)
    dynamic_update_slice x12, local copies, waits for them, and re-layouts, subset_gradient(): gradient = lax.dynamic_update_slice(gradient, current + addition, place)  78.6 us
    gather x36, local copies, waits for them, and re-layouts  44.4 us
    ppermute x4, waiting for transfers between devices, shifted(): return lax.ppermute(shard, axis, pairs)  30.6 us
    add x10, other arithmetic, subset_gradient(): gradient = lax.dynamic_update_slice(gradient, current + addition, place)  18.4 us
    dot_general x4, matrix products, right_multiply(): jnp.einsum('bjk,kl->bjl', data_re, matrix_re, precision=lax.Precision.HIG...  15.9 us
    dot_general x4, matrix products, right_multiply(): jnp.einsum('bjk,kl->bjl', data_re, matrix_im, precision=lax.Precision.HIG...  15.9 us
    dot_general x4, matrix products, left_multiply(): jnp.einsum('jk,bkl->bjl', matrix_im, data_im, precision=lax.Precision.HIG...  15.1 us
    dot_general x4, matrix products, right_multiply(): jnp.einsum('bjk,kl->bjl', data_im, matrix_im, precision=lax.Precision.HIG...  15.1 us
  transfers between devices with their start and end apart: 8, of which 6 were waited for; matrix products, arithmetic and copies ran while one was open for 2% of the time, Pallas kernels for 0%

commit v1 on v0

v1 whole, which is shorter than its diff:
```python
import functools

import jax
import jax.numpy as jnp
import numpy as np
from jax import lax
from jax.experimental import pallas as pl
from jax.experimental.pallas import tpu as pltpu
from jax.sharding import PartitionSpec as P

HALO = 128
FLOOR_VALUE = 0.5
LANES = 128


def shifted(shard, axis, by):
    count = lax.axis_size(axis)
    pairs = [(i, i + by) for i in range(count) if 0 <= i + by < count]
    return lax.ppermute(shard, axis, pairs)


def tables(window):
    half = window // 2
    n = np.arange(half)
    k = np.arange(half)
    swapped = np.roll(k, -(half // 2))

    def real_form(frequency):
        angle = 2.0 * np.pi * ((n[:, None] * frequency[None, :]) % window) / window
        c = np.cos(angle) / np.sqrt(window)
        s = np.sin(angle) / np.sqrt(window)
        return np.block([[c, -s], [s, c]])

    def split(matrix):
        high = matrix.astype(np.float32).astype(jnp.bfloat16)
        low = (matrix - high.astype(np.float64)).astype(jnp.bfloat16)
        return np.stack([high, low])

    even, odd, odd_swapped = real_form(2 * k), real_form(2 * k + 1), real_form(2 * swapped + 1)
    return np.stack([split(m) for m in (even, odd_swapped, even.T, odd_swapped.T, odd.T, odd)])


def split_high_low(x):
    high = x.astype(jnp.bfloat16)
    low = (x - high.astype(jnp.float32)).astype(jnp.bfloat16)
    return high, low


def copies(pairs, sems):
    started = []
    for number, (source, target) in enumerate(pairs):
        copy = pltpu.make_async_copy(source, target, sems.at[number])
        copy.start()
        started.append(copy)
    return started


def process_slots(
    row_first, row_last, starts_ref, live_ref, scale_ref, probe_ref, tables_ref, amplitudes,
    extended, total, scratch,
):
    (probe_rolled, wave, side_even, side_odd, block_u, block_v) = scratch
    window = probe_ref.shape[1]
    half = window // 2
    slots = amplitudes.shape[0] // 2

    def chosen(index):
        subset = index // slots
        row = starts_ref[2 * index]
        return (index - subset * slots < live_ref[subset]) & (row >= row_first) & (row <= row_last)

    lane = lax.broadcasted_iota(jnp.int32, (half, LANES), 1)
    to_even_first = jnp.where(lane < half // 2, 2 * lane, 2 * lane - half + 1)
    to_odd_first = jnp.where(lane < half // 2, 2 * lane + 1, 2 * lane - half)
    lower = lane < half // 2

    def tall(block):
        high, low = block[:window], block[window:]
        return jnp.concatenate([high, high, low], axis=0)

    def wide(sides):
        high, low = sides[:, :window], sides[:, window:]
        return jnp.concatenate([high, high, low], axis=1)

    def right(sides, number):
        high, low = tables_ref[number, 0], tables_ref[number, 1]
        return jnp.dot(wide(sides), jnp.concatenate([high, low, high], axis=0),
                       preferred_element_type=jnp.float32)

    def left(number, block):
        high, low = tables_ref[number, 0], tables_ref[number, 1]
        return jnp.dot(jnp.concatenate([high, low, high], axis=1), tall(block),
                       preferred_element_type=jnp.float32)

    def process(index):
        row = starts_ref[2 * index]
        column = starts_ref[2 * index + 1]
        tile = column // LANES
        offset = column - tile * LANES
        last_tile = jnp.minimum(tile + 2, extended.shape[1] - 1)
        at = pl.ds(row, window)
        moved = lax.broadcasted_iota(jnp.int32, (window, LANES), 1) < offset

        for part in range(2):
            first = pltpu.roll(probe_ref[part, :, :LANES], offset, 1)
            second = pltpu.roll(probe_ref[part, :, LANES:], offset, 1)
            probe_rolled[part, 0] = jnp.where(moved, second, first)
            probe_rolled[part, 1] = jnp.where(moved, first, second)
        for side in range(2):
            if side == 0:
                view = [
                    jnp.where(moved, extended[p, last_tile, at, :], extended[p, tile, at, :])
                    for p in range(2)
                ]
            else:
                view = [extended[p, tile + 1, at, :] for p in range(2)]
            p_re, p_im = probe_rolled[0, side], probe_rolled[1, side]
            wave[0, side] = p_re * view[0] - p_im * view[1]
            wave[1, side] = p_re * view[1] + p_im * view[0]
        for part in range(2):
            for sides, sign in ((side_even, 1), (side_odd, -1)):
                x = wave[part, 0] + wave[part, 1] if sign > 0 else wave[part, 0] - wave[part, 1]
                high, low = split_high_low(x)
                sides[:, part * LANES:(part + 1) * LANES] = high
                sides[:, window + part * LANES:window + (part + 1) * LANES] = low
        for number, sides in ((0, side_even), (1, side_odd)):
            y = right(sides, number)
            upper, under = y[:half], y[half:]
            to = slice(number * LANES, (number + 1) * LANES)
            for block, x in ((block_u, upper + under), (block_v, upper - under)):
                high, low = split_high_low(x)
                for part in range(2):
                    lanes = slice(part * LANES, (part + 1) * LANES)
                    block[part * half:(part + 1) * half, to] = high[:, lanes]
                    block[window + part * half:window + (part + 1) * half, to] = low[:, lanes]

        for number, block in ((0, block_u), (1, block_v)):
            z = left(2 + 2 * number, block)
            z_re, z_im = z[:half], z[half:]
            picked = [amplitudes[index, t, pl.ds(number, half, stride=2), :] for t in range(2)]
            g0 = jnp.take_along_axis(picked[0], to_even_first, axis=1)
            g1 = jnp.take_along_axis(picked[1], to_odd_first, axis=1)
            for t, amplitude in ((0, jnp.where(lower, g0, g1)), (1, jnp.where(lower, g1, g0))):
                lanes = slice(t * LANES, (t + 1) * LANES)
                a, b = z_re[:, lanes], z_im[:, lanes]
                power = jnp.maximum(a * a + b * b, FLOOR_VALUE * FLOOR_VALUE)
                ratio = amplitude * lax.rsqrt(power)
                for part, x in ((0, a * ratio), (1, b * ratio)):
                    high, low = split_high_low(x)
                    block[part * half:(part + 1) * half, lanes] = high
                    block[window + part * half:window + (part + 1) * half, lanes] = low
        p, q = left(0, block_u), left(5, block_v)
        for rows_half, x in ((0, p + q), (1, p - q)):
            high, low = split_high_low(x)
            to = slice(rows_half * half, (rows_half + 1) * half)
            for number, sides in ((0, side_even), (1, side_odd)):
                lanes = slice(number * LANES, (number + 1) * LANES)
                for part in range(2):
                    of = slice(part * half, (part + 1) * half)
                    sides[to, part * LANES:(part + 1) * LANES] = high[of, lanes]
                    sides[to, window + part * LANES:window + (part + 1) * LANES] = low[of, lanes]
        p, q = right(side_even, 2), right(side_odd, 3)
        scale = scale_ref[:1]
        for side, x in ((0, p + q), (1, p - q)):
            d_re = (x[:, :LANES] - wave[0, side]) * scale
            d_im = (x[:, LANES:] - wave[1, side]) * scale
            p_re, p_im = probe_rolled[0, side], probe_rolled[1, side]
            g = (p_re * d_re + p_im * d_im, p_re * d_im - p_im * d_re)
            for part in range(2):
                if side == 0:
                    total[part, tile, at, :] += jnp.where(moved, 0.0, g[part])
                    total[part, last_tile, at, :] += jnp.where(moved, g[part], 0.0)
                else:
                    total[part, tile + 1, at, :] += g[part]

    def step(index, carry):
        @pl.when(chosen(index))
        def _():
            process(index)

        return carry

    lax.fori_loop(0, 2 * slots, step, 0)


def setup_kernel(
    center, measured_ref, probe_in, tables_in, extended, total, amplitudes, scale, probe, tables,
    sems,
):
    own = pl.ds(HALO, center.shape[1])
    tiles = extended.shape[1]
    subsets, slots = measured_ref.shape[2:4]
    started = copies(
        [(probe_in, probe)]
        + [(center.at[part, :, pl.ds(tile * LANES, LANES)], extended.at[part, tile + 1, own, :])
           for part in range(2) for tile in range(tiles - 2)]
        + [(tables_in, tables)]
        + [(measured_ref.at[0, 0, subset, slot, :, pl.ds(tile * LANES, LANES)],
            amplitudes.at[subset * slots + slot, tile])
           for subset in range(subsets) for slot in range(slots) for tile in range(2)],
        sems)
    total[...] = jnp.zeros_like(total)
    started[0].wait()
    squared = probe[0] * probe[0] + probe[1] * probe[1]
    scale[...] = jnp.broadcast_to(1.0 / jnp.max(squared, keepdims=True), scale.shape)
    for copy in started[1:]:
        copy.wait()


def slots_kernel(
    row_first, row_last, parts, outputs, starts_ref, live_ref, scale_ref, probe_ref, tables_ref,
    amplitudes, *refs,
):
    arrived, refs = refs[:len(parts)], refs[len(parts) + 2:]
    extended, total, *refs = refs
    outs, scratch = refs[:len(outputs)], refs[len(outputs):]
    for ref, (row, rows, first) in zip(arrived, parts):
        for part in range(2):
            for tile in range(ref.shape[2] // LANES):
                extended[part, first + tile, row:row + rows, :] = (
                    ref[part, :, tile * LANES:(tile + 1) * LANES])
    process_slots(row_first, row_last, starts_ref, live_ref, scale_ref, probe_ref, tables_ref,
                  amplitudes, extended, total, scratch)
    for ref, (row, rows, first, with_object) in zip(outs, outputs):
        for part in range(2):
            for tile in range(ref.shape[2] // LANES):
                value = total[part, first + tile, row:row + rows, :]
                if with_object:
                    value = value + extended[part, first + tile, row:row + rows, :]
                ref[part, :, tile * LANES:(tile + 1) * LANES] = value


SMEM = pl.BlockSpec(memory_space=pltpu.SMEM)
VMEM = pl.BlockSpec(memory_space=pltpu.VMEM)
ANY = pl.BlockSpec(memory_space=pl.ANY)
HBM = pl.BlockSpec(memory_space=pltpu.HBM)
MIB = 1024 * 1024


def run_slots(row_range, common, extended, total, arrived, parts, outputs, out_shapes):
    window = common[3].shape[1]
    f32, bf16 = jnp.float32, jnp.bfloat16
    n = len(common) + len(arrived)
    return pl.pallas_call(
        functools.partial(slots_kernel, *row_range, parts, outputs),
        out_shape=[pltpu.VMEM(shape, f32)
                   for shape in [extended.shape, total.shape] + out_shapes],
        in_specs=[SMEM, SMEM] + [VMEM] * (n),
        out_specs=[VMEM] * (2 + len(out_shapes)),
        input_output_aliases={n: 0, n + 1: 1},
        scratch_shapes=[
            pltpu.VMEM((2, 2, window, LANES), f32),
            pltpu.VMEM((2, 2, window, LANES), f32),
            pltpu.VMEM((window, 2 * window), bf16),
            pltpu.VMEM((window, 2 * window), bf16),
            pltpu.VMEM((2 * window, window), bf16),
            pltpu.VMEM((2 * window, window), bf16),
        ],
        compiler_params=pltpu.CompilerParams(vmem_limit_bytes=12 * MIB),
        cost_estimate=pl.CostEstimate(
            flops=4 * 24 * 2 * window ** 3, bytes_accessed=12 * MIB, transcendentals=0),
    )(*common, *arrived, extended, total)


def tail_kernel(body, from_left, from_right, from_below, out, head, kept, sems):
    height, width = body.shape[1:]
    kept[...] = body[...]
    kept[:, :, :HALO] += from_left[...]
    kept[:, :, width - HALO:] += from_right[...]
    kept[:, height - HALO:, :] += from_below[...]
    rows = pl.ds(HALO, height - HALO)
    started = copies([(kept.at[part, rows, :], out.at[part, rows, :]) for part in range(2)], sems)
    head[...] = kept[:, :HALO, :]
    for copy in started:
        copy.wait()


def head_kernel(head, from_above, old, out, kept, sems):
    kept[...] = head[...] + from_above[...]
    rows = pl.ds(0, HALO)
    for copy in copies([(kept.at[part], out.at[part, rows, :]) for part in range(2)], sems):
        copy.wait()


def update(transmission, probe_wave, positions, counts, measured):
    height, width = transmission.shape[1:]
    window = probe_wave.shape[1]
    slots = measured.shape[3]
    tiles = (width + 2 * HALO) // LANES
    whole = (2, tiles, height + 2 * HALO, LANES)
    wide_rim, small_rim, side = (2, HALO, width), (2, HALO, HALO), (2, height, HALO)
    above = shifted(transmission[:, height - HALO:, :], "narrow", 1)
    left = shifted(transmission[:, :, width - HALO:], "wide", 1)
    right = shifted(transmission[:, :, :HALO], "wide", -1)
    upper = transmission[:, :HALO, :]

    table = jnp.asarray(tables(window))
    f32 = jnp.float32
    loads = 2 + 2 * (tiles - 2) + 4 * slots
    extended, total, amplitudes, scale, probe, table = pl.pallas_call(
        setup_kernel, name="setup",
        out_shape=[
            pltpu.VMEM(whole, f32), pltpu.VMEM(whole, f32),
            pltpu.VMEM((2 * slots, 2, window, LANES), f32), pltpu.VMEM((8, LANES), f32),
            pltpu.VMEM(probe_wave.shape, f32), pltpu.VMEM(table.shape, table.dtype)],
        in_specs=[HBM] * 4, out_specs=[VMEM] * 6,
        scratch_shapes=[pltpu.SemaphoreType.DMA((loads,))],
        compiler_params=pltpu.CompilerParams(vmem_limit_bytes=12 * MIB),
        cost_estimate=pl.CostEstimate(
            flops=0, bytes_accessed=8 * MIB, transcendentals=0),
    )(*(pltpu.with_memory_space_constraint(x, pltpu.HBM)
        for x in (transmission, measured, probe_wave, table)))
    common = (positions.reshape(-1), counts.reshape(-1), scale, probe, table, amplitudes)

    extended, total = run_slots(
        (HALO, height + HALO - window), common, extended, total,
        (left, right), ((HALO, height, 0), (HALO, height, tiles - 1)), (), [])

    above, total, upper = lax.optimization_barrier((above, total, upper))
    below = shifted(upper, "narrow", -1)
    above_l = shifted(above[:, :, width - HALO:], "wide", 1)
    above_r = shifted(above[:, :, :HALO], "wide", -1)

    def rim(row):
        return ((row, HALO, 1), (row, HALO, 0), (row, HALO, tiles - 1))

    def rim_out(row):
        return tuple((*piece, False) for piece in rim(row))

    rims = [wide_rim, small_rim, small_rim]
    extended, total, up, up_l, up_r = run_slots(
        (0, HALO - 1), common, extended, total,
        (above, above_l, above_r), rim(0), rim_out(0), rims)

    def fold_columns(center, from_left, from_right):
        center = center.at[:, :, :HALO].add(from_left)
        return center.at[:, :, width - HALO:].add(from_right)

    up = fold_columns(up, shifted(up_r, "wide", 1), shifted(up_l, "wide", -1))
    from_below = shifted(up, "narrow", -1)

    below, total = lax.optimization_barrier((below, total))
    below_l = shifted(below[:, :, width - HALO:], "wide", 1)
    below_r = shifted(below[:, :, :HALO], "wide", -1)
    last = height + HALO
    extended, total, down, down_l, down_r, body, body_l, body_r = run_slots(
        (height + HALO - window + 1, height), common, extended, total,
        (below, below_l, below_r), rim(last),
        rim_out(last) + ((HALO, height, 1, True), (HALO, height, 0, False),
                         (HALO, height, tiles - 1, False)),
        rims + [(2, height, width), side, side])
    down = fold_columns(down, shifted(down_r, "wide", 1), shifted(down_l, "wide", -1))
    from_above = shifted(down, "narrow", 1)
    from_left = shifted(body_r, "wide", 1)
    from_right = shifted(body_l, "wide", -1)

    out, head = pl.pallas_call(
        tail_kernel, name="tail",
        out_shape=[jax.ShapeDtypeStruct((2, height, width), f32),
                   pltpu.VMEM(wide_rim, f32)],
        in_specs=[VMEM] * 4, out_specs=[ANY, VMEM],
        scratch_shapes=[pltpu.VMEM((2, height, width), f32), pltpu.SemaphoreType.DMA((2,))],
        compiler_params=pltpu.CompilerParams(vmem_limit_bytes=8 * MIB),
    )(body, from_left, from_right, from_below)
    return pl.pallas_call(
        head_kernel, name="head",
        out_shape=jax.ShapeDtypeStruct((2, height, width), f32),
        in_specs=[VMEM, VMEM, ANY], out_specs=ANY,
        input_output_aliases={2: 0},
        scratch_shapes=[pltpu.VMEM(wide_rim, f32), pltpu.SemaphoreType.DMA((2,))],
        compiler_params=pltpu.CompilerParams(vmem_limit_bytes=4 * MIB),
    )(head, from_above, out)


def solution(mesh):
    in_specs = (
        P(None, "narrow", "wide"),
        P(),
        P("narrow", "wide", None, None, None),
        P("narrow", "wide", None),
        P("narrow", "wide", None, None, None, None),
    )
    out_specs = P(None, "narrow", "wide")
    return jax.shard_map(update, mesh=mesh, in_specs=in_specs, out_specs=out_specs, check_vma=False)
```

time: 413 us -> 99.6 us (0.24); the launches traced: 406 us -> 98.6 us
  local copies, waits for them, and re-layouts: 141 us -> 3.6 us
  matrix products: 120 us -> 0 us
  between operations: 46.6 us -> 0.32 us
  other arithmetic: 35.3 us -> 0.13 us
  starting transfers between devices: 23.8 us -> 54.2 us
  Pallas kernels: 0 us -> 23.1 us
  waiting for transfers between devices: 39.4 us -> 17.3 us
    dot_general x32 -> x0, matrix products: 120 us -> none  [the longest x4 15.9 us: right_multiply(): jnp.einsum('bjk,kl->bjl', data_re, matrix_re, precision=lax.Precision.HIG...]
    dynamic_update_slice x12 -> x0, local copies, waits for them, and re-layouts: 78.6 us -> none  [subset_gradient(): gradient = lax.dynamic_update_slice(gradient, current + addition, place)]
    gather x36 -> x0, local copies, waits for them, and re-layouts: 44.4 us -> none
    ppermute x4 -> x16, starting transfers between devices: 11.3 us -> 54.2 us  [shifted(): return lax.ppermute(shard, axis, pairs)]
    add x13 -> x0, other arithmetic: 27.3 us -> none  [the longest x10 18.4 us: subset_gradient(): gradient = lax.dynamic_update_slice(gradient, current + addition, place)]
    pallas_call x0 -> x6, Pallas kernels: none -> 23.1 us  [the longest x3 17.2 us: run_slots(): pl.pallas_call(functools.partial(slots_kernel, *row_range, parts, outputs...]
    ppermute x4 -> x16, waiting for transfers between devices: 30.6 us -> 17.3 us  [shifted(): return lax.ppermute(shard, axis, pairs)]
    ppermute x4 -> x0, starting transfers between devices: 12.5 us -> none  [the longest x2 7.51 us: with_halo(): before = lax.ppermute(last, axis, up)]
  transfers between devices with their start and end apart: 8 -> 16, of which waited for: 6 -> 5; matrix products, arithmetic and copies ran while one was open for 2% -> 2% of each run, Pallas kernels for 0% -> 23%
where the time goes in v1:
time: 99.6 us; the launch traced here: 98.6 us
  starting transfers between devices  54.2 us (54%)
  Pallas kernels  23.1 us (23%)
  waiting for transfers between devices  17.3 us (17%)
  local copies, waits for them, and re-layouts  3.6 us (4%)
    ppermute x16, starting transfers between devices, shifted(): return lax.ppermute(shard, axis, pairs)  54.2 us
    ppermute x16, waiting for transfers between devices, shifted(): return lax.ppermute(shard, axis, pairs)  17.3 us
    pallas_call x3, Pallas kernels, run_slots(): pl.pallas_call(functools.partial(slots_kernel, *row_range, parts, outputs...  17.2 us
    pallas_call x1, Pallas kernels, update(): pl.pallas_call(setup_kernel, name='setup', out_shape=[pltpu.VMEM(whole, f...  3.56 us
    slice x1, local copies, waits for them, and re-layouts, update(): right = shifted(transmission[:, :, :HALO], 'wide', -1)  2.09 us
  transfers between devices with their start and end apart: 16, of which 5 were waited for; matrix products, arithmetic and copies ran while one was open for 2% of the time, Pallas kernels for 23%

profile of v1, /device:TPU:25, one launch (start us, length us, event | category | flops | bytes accessed | tf_op | source)
XLA Modules:
  0.0 98.6 jit_solution(15468292081320899928)
XLA Ops:
  0.0 2.1 %fusion.3 = (f32[2,512,128]{2,1,0:T(8,128)}, f32[2,512,128]{2,1,0:T(8,128)S(1)}) fusion(f32[2,512,512]{2,1,0:T(8,128)} %center.1), kind=kLoop, calls=%fused_computation.7 | loop fusion | bytes 2097152 | tf_op jit(solution)/shard_map/slice | solution.py:294
  2.1 2.6 %collective-permute-start.2 = (f32[2,512,128]{2,1,0:T(8,128)}, f32[2,512,128]{2,1,0:T(8,128)S(1)}, u32[]{:S(2)}, u32[]{:S(2)}) collective-permute-start(f32[2,512,128]{2,1,0:T(8,128)} %get-tuple-element.107), channel_id=1, source_target_pairs={{8,0},{16,8},{24,16},{9,1},{17,9},{25,17},{10,2},{18,10},{26,18},{... | collective-permute-start | bytes 1572872 | tf_op jit(solution)/shard_map/ppermute | solution.py:19
  4.7 3.0 %collective-permute-start.1 = (f32[2,512,128]{2,1,0:T(8,128)S(1)}, f32[2,512,128]{2,1,0:T(8,128)S(1)}, u32[]{:S(2)}, u32[]{:S(2)}) collective-permute-start(f32[2,512,128]{2,1,0:T(8,128)S(1)} %get-tuple-element.108), channel_id=1, source_target_pairs={{0,8},{8,16},{16,24},{1,9},{9,17},{17,25},{2,10},{10,18},{18,26},{... | collective-permute-start | bytes 1572872 | tf_op jit(solution)/shard_map/ppermute | solution.py:19
  7.7 1.3 %fusion.2 = (f32[2,128,512]{2,1,0:T(8,128)S(1)}, f32[2,128,512]{2,1,0:T(8,128)S(1)}) fusion(f32[2,512,512]{2,1,0:T(8,128)} %center.1), kind=kLoop, calls=%fused_computation.6 | loop fusion | bytes 2097152 | tf_op jit(solution)/shard_map/slice | solution.py:295
  9.0 3.1 %collective-permute-start = (f32[2,128,512]{2,1,0:T(8,128)S(1)}, f32[2,128,512]{2,1,0:T(8,128)S(1)}, u32[]{:S(2)}, u32[]{:S(2)}) collective-permute-start(f32[2,128,512]{2,1,0:T(8,128)S(1)} %get-tuple-element.106), channel_id=1, source_target_pairs={{0,1},{1,2},{2,3},{3,4},{4,5},{5,6},{6,7},{8,9},{9,10},{10,11},{11... | collective-permute-start | bytes 1572872 | tf_op jit(solution)/shard_map/ppermute | solution.py:19
  12.3 3.6 %setup.1 = (f32[2,6,768,128]{3,2,1,0:T(8,128)S(1)}, f32[2,6,768,128]{3,2,1,0:T(8,128)S(1)}, f32[12,2,256,128]{3,2,1,0:T(8,128)S(1)}, f32[8,128]{1,0:T(8,128)S(1)...) custom-call(f32[2,512,512]{2,1,0:T(8,128)} %center.1, f32[1,1,2,6,256,256]{5,4,3,2,1,0:T(8,128)} %measured_ref.1, ...), custom_call_target="tpu_custom_call" | custom-call | bytes 8388608 | tf_op jit(solution)/shard_map/setup/pallas_call | solution.py:300
  15.9 12.9 %shard_map.64 = (f32[2,6,768,128]{3,2,1,0:T(8,128)S(1)}, f32[2,6,768,128]{3,2,1,0:T(8,128)S(1)}) custom-call(s32[24]{0:T(128)S(1)} %reshape.122.starts_ref, s32[2]{0:T(128)S(1)} %bitcast.1, f32[8,128]{1,0:T(8,128)S(1)} %get-tuple-element.79.scale_ref, f32[2,256,256]{2,1,0:T(8,128)S(1)} %get-tuple-element.80.probe_ref, ...), custom_call_target="tpu_custom_call", output_to_operand_aliasing={{0}: (8, {}), {1}: (9, {})} | custom-call | flops 3221225472 | bytes 12582912 | tf_op jit(solution)/shard_map/pallas_call | solution.py:244
  28.9 1.9 %collective-permute-start.3 = (f32[2,128,512]{2,1,0:T(8,128)S(1)}, f32[2,128,512]{2,1,0:T(8,128)S(1)}, u32[]{:S(2)}, u32[]{:S(2)}) collective-permute-start(f32[2,128,512]{2,1,0:T(8,128)S(1)} %get-tuple-element.86), channel_id=1, source_target_pairs={{1,0},{2,1},{3,2},{4,3},{5,4},{6,5},{7,6},{9,8},{10,9},{11,10},{12... | collective-permute-start | bytes 1572872 | tf_op jit(solution)/shard_map/ppermute | solution.py:19
  30.8 1.9 %collective-permute-start.5 = (f32[2,128,128]{2,1,0:T(8,128)S(1)}, f32[2,128,128]{2,1,0:T(8,128)S(1)}, u32[]{:S(2)}, u32[]{:S(2)}) collective-permute-start(f32[2,128,128]{2,1,0:T(8,128)S(1)} %get-tuple-element.111), channel_id=1, source_target_pairs={{8,0},{16,8},{24,16},{9,1},{17,9},{25,17},{10,2},{18,10},{26,18},{... | collective-permute-start | bytes 393224 | tf_op jit(solution)/shard_map/ppermute | solution.py:19
  32.8 3.6 %collective-permute-start.4 = (f32[2,128,128]{2,1,0:T(8,128)S(1)}, f32[2,128,128]{2,1,0:T(8,128)S(1)}, u32[]{:S(2)}, u32[]{:S(2)}) collective-permute-start(f32[2,128,128]{2,1,0:T(8,128)S(1)} %get-tuple-element.112), channel_id=1, source_target_pairs={{0,8},{8,16},{16,24},{1,9},{9,17},{17,25},{2,10},{10,18},{18,26},{... | collective-permute-start | bytes 393224 | tf_op jit(solution)/shard_map/ppermute | solution.py:19
  38.3 3.0 %shard_map.65 = (f32[2,6,768,128]{3,2,1,0:T(8,128)S(1)}, f32[2,6,768,128]{3,2,1,0:T(8,128)S(1)}, f32[2,128,512]{2,1,0:T(8,128)S(1)}, f32[2,128,128]{2,1,0:T(8,128)S(1)}, f32[2,128,128]{2,1,0:T(8,128)S(1)}) custom-call(s32[24]{0:T(128)S(1)} %reshape.122.starts_ref, s32[2]{0:T(128)S(1)} %bitcast.2, ...), custom_call_target="tpu_custom_call", output_to_operand_aliasing={{0}: (9, {}), {1}: (10, {})} | custom-call | flops 3221225472 | bytes 12582912 | tf_op jit(solution)/shard_map/pallas_call | solution.py:244
  41.3 6.4 %collective-permute-start.10 = (f32[2,128,128]{2,1,0:T(8,128)S(1)}, f32[2,128,128]{2,1,0:T(8,128)S(1)}, u32[]{:S(2)}, u32[]{:S(2)}) collective-permute-start(f32[2,128,128]{2,1,0:T(8,128)S(1)} %get-tuple-element.98), channel_id=1, source_target_pairs={{0,8},{8,16},{16,24},{1,9},{9,17},{17,25},{2,10},{10,18},{18,26},{... | collective-permute-start | bytes 393224 | tf_op jit(solution)/shard_map/ppermute | solution.py:19
  47.7 1.9 %collective-permute-start.11 = (f32[2,128,128]{2,1,0:T(8,128)S(1)}, f32[2,128,128]{2,1,0:T(8,128)S(1)}, u32[]{:S(2)}, u32[]{:S(2)}) collective-permute-start(f32[2,128,128]{2,1,0:T(8,128)S(1)} %get-tuple-element.99), channel_id=1, source_target_pairs={{8,0},{16,8},{24,16},{9,1},{17,9},{25,17},{10,2},{18,10},{26,18},{... | collective-permute-start | bytes 393224 | tf_op jit(solution)/shard_map/ppermute | solution.py:19
  49.6 1.9 %collective-permute-start.7 = (f32[2,128,128]{2,1,0:T(8,128)S(1)}, f32[2,128,128]{2,1,0:T(8,128)S(1)}, u32[]{:S(2)}, u32[]{:S(2)}) collective-permute-start(f32[2,128,128]{2,1,0:T(8,128)S(1)} %get-tuple-element.109), channel_id=1, source_target_pairs={{8,0},{16,8},{24,16},{9,1},{17,9},{25,17},{10,2},{18,10},{26,18},{... | collective-permute-start | bytes 393224 | tf_op jit(solution)/shard_map/ppermute | solution.py:19
  51.6 3.6 %collective-permute-start.6 = (f32[2,128,128]{2,1,0:T(8,128)S(1)}, f32[2,128,128]{2,1,0:T(8,128)S(1)}, u32[]{:S(2)}, u32[]{:S(2)}) collective-permute-start(f32[2,128,128]{2,1,0:T(8,128)S(1)} %get-tuple-element.110), channel_id=1, source_target_pairs={{0,8},{8,16},{16,24},{1,9},{9,17},{17,25},{2,10},{10,18},{18,26},{... | collective-permute-start | bytes 393224 | tf_op jit(solution)/shard_map/ppermute | solution.py:19
  57.1 1.3 %shard_map.66 = (f32[2,6,768,128]{3,2,1,0:T(8,128)S(1)}, f32[2,6,768,128]{3,2,1,0:T(8,128)S(1)}, f32[2,128,512]{2,1,0:T(8,128)S(1)}, f32[2,128,128]{2,1,0:T(8,12...) custom-call(s32[24]{0:T(128)S(1)} %reshape.122.starts_ref, ...), custom_call_target="tpu_custom_call", output_to_operand_aliasing={{0}: (9, {}), {1}: (10, {})} | custom-call | flops 3221225472 | bytes 12582912 | tf_op jit(solution)/shard_map/pallas_call | solution.py:244
  58.5 10.4 %collective-permute-start.13 = (f32[2,128,128]{2,1,0:T(8,128)S(1)}, f32[2,128,128]{2,1,0:T(8,128)S(1)}, u32[]{:S(2)}, u32[]{:S(2)}) collective-permute-start(f32[2,128,128]{2,1,0:T(8,128)S(1)} %get-tuple-element.102), channel_id=1, source_target_pairs={{0,8},{8,16},{16,24},{1,9},{9,17},{17,25},{2,10},{10,18},{18,26},{... | collective-permute-start | bytes 393224 | tf_op jit(solution)/shard_map/ppermute | solution.py:19
  68.9 1.9 %collective-permute-start.12 = (f32[2,128,512]{2,1,0:T(8,128)S(1)}, f32[2,128,512]{2,1,0:T(8,128)S(1)}, u32[]{:S(2)}, u32[]{:S(2)}) collective-permute-start(f32[2,128,512]{2,1,0:T(8,128)S(1)} %fusion.1), channel_id=1, source_target_pairs={{1,0},{2,1},{3,2},{4,3},{5,4},{6,5},{7,6},{9,8},{10,9},{11,10},{12... | collective-permute-start | bytes 1572872 | tf_op jit(solution)/shard_map/ppermute | solution.py:19
  70.8 1.9 %collective-permute-start.14 = (f32[2,128,128]{2,1,0:T(8,128)S(1)}, f32[2,128,128]{2,1,0:T(8,128)S(1)}, u32[]{:S(2)}, u32[]{:S(2)}) collective-permute-start(f32[2,128,128]{2,1,0:T(8,128)S(1)} %get-tuple-element.103), channel_id=1, source_target_pairs={{8,0},{16,8},{24,16},{9,1},{17,9},{25,17},{10,2},{18,10},{26,18},{... | collective-permute-start | bytes 393224 | tf_op jit(solution)/shard_map/ppermute | solution.py:19
  72.8 3.6 %collective-permute-start.8 = (f32[2,512,128]{2,1,0:T(8,128)S(1)}, f32[2,512,128]{2,1,0:T(8,128)S(1)}, u32[]{:S(2)}, u32[]{:S(2)}) collective-permute-start(f32[2,512,128]{2,1,0:T(8,128)S(1)} %get-tuple-element.95), channel_id=1, source_target_pairs={{0,8},{8,16},{16,24},{1,9},{9,17},{17,25},{2,10},{10,18},{18,26},{... | collective-permute-start | bytes 1572872 | tf_op jit(solution)/shard_map/ppermute | solution.py:19
  76.4 1.9 %collective-permute-start.9 = (f32[2,512,128]{2,1,0:T(8,128)S(1)}, f32[2,512,128]{2,1,0:T(8,128)S(1)}, u32[]{:S(2)}, u32[]{:S(2)}) collective-permute-start(f32[2,512,128]{2,1,0:T(8,128)S(1)} %get-tuple-element.96), channel_id=1, source_target_pairs={{8,0},{16,8},{24,16},{9,1},{17,9},{25,17},{10,2},{18,10},{26,18},{... | collective-permute-start | bytes 1572872 | tf_op jit(solution)/shard_map/ppermute | solution.py:19
  78.5 4.3 %collective-permute-start.15 = (f32[2,128,512]{2,1,0:T(8,128)S(1)}, f32[2,128,512]{2,1,0:T(8,128)S(1)}, u32[]{:S(2)}, u32[]{:S(2)}) collective-permute-start(f32[2,128,512]{2,1,0:T(8,128)S(1)} %fusion), channel_id=1, source_target_pairs={{0,1},{1,2},{2,3},{3,4},{4,5},{5,6},{6,7},{8,9},{9,10},{10,11},{11... | collective-permute-start | bytes 1572872 | tf_op jit(solution)/shard_map/ppermute | solution.py:19
  82.8 13.5 %collective-permute-done.12.from_below = f32[2,128,512]{2,1,0:T(8,128)S(1)} collective-permute-done((f32[2,128,512]{2,1,0:T(8,128)S(1)}, f32[2,128,512]{2,1,0:T(8,128)S(1)}, u32[]{:S(2)}, u32[]{:S(2)}) %collective-permute-start.12) | collective-permute-done | bytes 524320 | tf_op jit(solution)/shard_map/ppermute | solution.py:19
  96.3 1.5 %tail.1 = (f32[2,512,512]{2,1,0:T(8,128)}, f32[2,128,512]{2,1,0:T(8,128)S(1)}) custom-call(f32[2,512,512]{2,1,0:T(8,128)S(1)} %get-tuple-element.94.body, f32[2,512,128]{2,1,0:T(8,128)S(1)} %collective-permute-done.8.from_left, f32[2,512,128]{2,1,0:T(8,128)S(1)} %collective-permute-done.9.from_right, f32[2,128,512]{2,1,0:T(8,128)S(1)} %collective-permute-done.12.from_below), custom_call_target="tpu_custom_call" | custom-call | tf_op jit(solution)/shard_map/tail/pallas_call | solution.py:357
  (28 shorter events, 5.1 us)
Async XLA Ops:
  0.0 12.1 %copy-start.1 = (s32[1,1,2,6,2]{3,4,2,1,0:T(2,128)S(1)}, s32[1,1,2,6,2]{3,4,2,1,0:T(2,128)}, u32[]{:S(2)}) copy-start(s32[1,1,2,6,2]{3,4,2,1,0:T(2,128)} %param.16) | copy-start | bytes 292
  2.1 13.8 %collective-permute-start.2 = (f32[2,512,128]{2,1,0:T(8,128)}, f32[2,512,128]{2,1,0:T(8,128)S(1)}, u32[]{:S(2)}, u32[]{:S(2)}) collective-permute-start(f32[2,512,128]{2,1,0:T(8,128)} %get-tuple-element.107), channel_id=1, source_target_pairs={{8,0},{16,8},{24,16},{9,1},{17,9},{25,17},{10,2},{18,10},{26,18},{... | collective-permute-start | bytes 1572872 | tf_op jit(solution)/shard_map/ppermute | solution.py:19
  4.7 11.3 %collective-permute-start.1 = (f32[2,512,128]{2,1,0:T(8,128)S(1)}, f32[2,512,128]{2,1,0:T(8,128)S(1)}, u32[]{:S(2)}, u32[]{:S(2)}) collective-permute-start(f32[2,512,128]{2,1,0:T(8,128)S(1)} %get-tuple-element.108), channel_id=1, source_target_pairs={{0,8},{8,16},{16,24},{1,9},{9,17},{17,25},{2,10},{10,18},{18,26},{... | collective-permute-start | bytes 1572872 | tf_op jit(solution)/shard_map/ppermute | solution.py:19
  9.0 19.9 %collective-permute-start = (f32[2,128,512]{2,1,0:T(8,128)S(1)}, f32[2,128,512]{2,1,0:T(8,128)S(1)}, u32[]{:S(2)}, u32[]{:S(2)}) collective-permute-start(f32[2,128,512]{2,1,0:T(8,128)S(1)} %get-tuple-element.106), channel_id=1, source_target_pairs={{0,1},{1,2},{2,3},{3,4},{4,5},{5,6},{6,7},{8,9},{9,10},{10,11},{11... | collective-permute-start | bytes 1572872 | tf_op jit(solution)/shard_map/ppermute | solution.py:19
  12.3 3.6 %copy-start = (s32[1,1,2]{2,1,0:T(1,128)S(1)}, s32[1,1,2]{2,1,0:T(1,128)}, u32[]{:S(2)}) copy-start(s32[1,1,2]{2,1,0:T(1,128)} %param.17) | copy-start | bytes 28
  28.9 20.7 %collective-permute-start.3 = (f32[2,128,512]{2,1,0:T(8,128)S(1)}, f32[2,128,512]{2,1,0:T(8,128)S(1)}, u32[]{:S(2)}, u32[]{:S(2)}) collective-permute-start(f32[2,128,512]{2,1,0:T(8,128)S(1)} %get-tuple-element.86), channel_id=1, source_target_pairs={{1,0},{2,1},{3,2},{4,3},{5,4},{6,5},{7,6},{9,8},{10,9},{11,10},{12... | collective-permute-start | bytes 1572872 | tf_op jit(solution)/shard_map/ppermute | solution.py:19
  30.8 6.6 %collective-permute-start.5 = (f32[2,128,128]{2,1,0:T(8,128)S(1)}, f32[2,128,128]{2,1,0:T(8,128)S(1)}, u32[]{:S(2)}, u32[]{:S(2)}) collective-permute-start(f32[2,128,128]{2,1,0:T(8,128)S(1)} %get-tuple-element.111), channel_id=1, source_target_pairs={{8,0},{16,8},{24,16},{9,1},{17,9},{25,17},{10,2},{18,10},{26,18},{... | collective-permute-start | bytes 393224 | tf_op jit(solution)/shard_map/ppermute | solution.py:19
  32.8 5.6 %collective-permute-start.4 = (f32[2,128,128]{2,1,0:T(8,128)S(1)}, f32[2,128,128]{2,1,0:T(8,128)S(1)}, u32[]{:S(2)}, u32[]{:S(2)}) collective-permute-start(f32[2,128,128]{2,1,0:T(8,128)S(1)} %get-tuple-element.112), channel_id=1, source_target_pairs={{0,8},{8,16},{16,24},{1,9},{9,17},{17,25},{2,10},{10,18},{18,26},{... | collective-permute-start | bytes 393224 | tf_op jit(solution)/shard_map/ppermute | solution.py:19
  41.3 13.9 %collective-permute-start.10 = (f32[2,128,128]{2,1,0:T(8,128)S(1)}, f32[2,128,128]{2,1,0:T(8,128)S(1)}, u32[]{:S(2)}, u32[]{:S(2)}) collective-permute-start(f32[2,128,128]{2,1,0:T(8,128)S(1)} %get-tuple-element.98), channel_id=1, source_target_pairs={{0,8},{8,16},{16,24},{1,9},{9,17},{17,25},{2,10},{10,18},{18,26},{... | collective-permute-start | bytes 393224 | tf_op jit(solution)/shard_map/ppermute | solution.py:19
  47.7 21.2 %collective-permute-start.11 = (f32[2,128,128]{2,1,0:T(8,128)S(1)}, f32[2,128,128]{2,1,0:T(8,128)S(1)}, u32[]{:S(2)}, u32[]{:S(2)}) collective-permute-start(f32[2,128,128]{2,1,0:T(8,128)S(1)} %get-tuple-element.99), channel_id=1, source_target_pairs={{8,0},{16,8},{24,16},{9,1},{17,9},{25,17},{10,2},{18,10},{26,18},{... | collective-permute-start | bytes 393224 | tf_op jit(solution)/shard_map/ppermute | solution.py:19
  49.6 6.3 %collective-permute-start.7 = (f32[2,128,128]{2,1,0:T(8,128)S(1)}, f32[2,128,128]{2,1,0:T(8,128)S(1)}, u32[]{:S(2)}, u32[]{:S(2)}) collective-permute-start(f32[2,128,128]{2,1,0:T(8,128)S(1)} %get-tuple-element.109), channel_id=1, source_target_pairs={{8,0},{16,8},{24,16},{9,1},{17,9},{25,17},{10,2},{18,10},{26,18},{... | collective-permute-start | bytes 393224 | tf_op jit(solution)/shard_map/ppermute | solution.py:19
  51.6 5.6 %collective-permute-start.6 = (f32[2,128,128]{2,1,0:T(8,128)S(1)}, f32[2,128,128]{2,1,0:T(8,128)S(1)}, u32[]{:S(2)}, u32[]{:S(2)}) collective-permute-start(f32[2,128,128]{2,1,0:T(8,128)S(1)} %get-tuple-element.110), channel_id=1, source_target_pairs={{0,8},{8,16},{16,24},{1,9},{9,17},{17,25},{2,10},{10,18},{18,26},{... | collective-permute-start | bytes 393224 | tf_op jit(solution)/shard_map/ppermute | solution.py:19
  58.5 19.9 %collective-permute-start.13 = (f32[2,128,128]{2,1,0:T(8,128)S(1)}, f32[2,128,128]{2,1,0:T(8,128)S(1)}, u32[]{:S(2)}, u32[]{:S(2)}) collective-permute-start(f32[2,128,128]{2,1,0:T(8,128)S(1)} %get-tuple-element.102), channel_id=1, source_target_pairs={{0,8},{8,16},{16,24},{1,9},{9,17},{17,25},{2,10},{10,18},{18,26},{... | collective-permute-start | bytes 393224 | tf_op jit(solution)/shard_map/ppermute | solution.py:19
  68.9 27.3 %collective-permute-start.12 = (f32[2,128,512]{2,1,0:T(8,128)S(1)}, f32[2,128,512]{2,1,0:T(8,128)S(1)}, u32[]{:S(2)}, u32[]{:S(2)}) collective-permute-start(f32[2,128,512]{2,1,0:T(8,128)S(1)} %fusion.1), channel_id=1, source_target_pairs={{1,0},{2,1},{3,2},{4,3},{5,4},{6,5},{7,6},{9,8},{10,9},{11,10},{12... | collective-permute-start | bytes 1572872 | tf_op jit(solution)/shard_map/ppermute | solution.py:19
  70.8 7.6 %collective-permute-start.14 = (f32[2,128,128]{2,1,0:T(8,128)S(1)}, f32[2,128,128]{2,1,0:T(8,128)S(1)}, u32[]{:S(2)}, u32[]{:S(2)}) collective-permute-start(f32[2,128,128]{2,1,0:T(8,128)S(1)} %get-tuple-element.103), channel_id=1, source_target_pairs={{8,0},{16,8},{24,16},{9,1},{17,9},{25,17},{10,2},{18,10},{26,18},{... | collective-permute-start | bytes 393224 | tf_op jit(solution)/shard_map/ppermute | solution.py:19
  72.8 23.5 %collective-permute-start.8 = (f32[2,512,128]{2,1,0:T(8,128)S(1)}, f32[2,512,128]{2,1,0:T(8,128)S(1)}, u32[]{:S(2)}, u32[]{:S(2)}) collective-permute-start(f32[2,512,128]{2,1,0:T(8,128)S(1)} %get-tuple-element.95), channel_id=1, source_target_pairs={{0,8},{8,16},{16,24},{1,9},{9,17},{17,25},{2,10},{10,18},{18,26},{... | collective-permute-start | bytes 1572872 | tf_op jit(solution)/shard_map/ppermute | solution.py:19
  76.4 19.8 %collective-permute-start.9 = (f32[2,512,128]{2,1,0:T(8,128)S(1)}, f32[2,512,128]{2,1,0:T(8,128)S(1)}, u32[]{:S(2)}, u32[]{:S(2)}) collective-permute-start(f32[2,512,128]{2,1,0:T(8,128)S(1)} %get-tuple-element.96), channel_id=1, source_target_pairs={{8,0},{16,8},{24,16},{9,1},{17,9},{25,17},{10,2},{18,10},{26,18},{... | collective-permute-start | bytes 1572872 | tf_op jit(solution)/shard_map/ppermute | solution.py:19
  78.5 19.3 %collective-permute-start.15 = (f32[2,128,512]{2,1,0:T(8,128)S(1)}, f32[2,128,512]{2,1,0:T(8,128)S(1)}, u32[]{:S(2)}, u32[]{:S(2)}) collective-permute-start(f32[2,128,512]{2,1,0:T(8,128)S(1)} %fusion), channel_id=1, source_target_pairs={{0,1},{1,2},{2,3},{3,4},{4,5},{5,6},{6,7},{8,9},{9,10},{10,11},{11... | collective-permute-start | bytes 1572872 | tf_op jit(solution)/shard_map/ppermute | solution.py:19

commit v2 on v1

v2 whole, which is shorter than its diff:
```python
import functools

import jax
import jax.numpy as jnp
import numpy as np
from jax import lax
from jax.experimental import pallas as pl
from jax.experimental.pallas import tpu as pltpu
from jax.sharding import PartitionSpec as P

HALO = 128
FLOOR_VALUE = 0.5
LANES = 128
PIECE = 32
HEAD = 2
EARLY = 4


NEAR, FAR = range(2)


def swapped(shard, axis, which):
    count = lax.axis_size(axis)
    pairs = [pair for i in range(which, count - 1, 2) for pair in ((i, i + 1), (i + 1, i))]
    return lax.ppermute(shard, axis, pairs)


def is_after(axis, which):
    odd = lax.rem(lax.axis_index(axis), 2)
    return odd if which == FAR else 1 - odd


def tables(window):
    half = window // 2
    n = np.arange(half)
    k = np.arange(half)
    swapped = np.roll(k, -(half // 2))

    def real_form(frequency):
        angle = 2.0 * np.pi * ((n[:, None] * frequency[None, :]) % window) / window
        c = np.cos(angle) / np.sqrt(window)
        s = np.sin(angle) / np.sqrt(window)
        return np.block([[c, -s], [s, c]])

    def split(matrix):
        high = matrix.astype(np.float32).astype(jnp.bfloat16)
        low = (matrix - high.astype(np.float64)).astype(jnp.bfloat16)
        return np.stack([high, low])

    even, odd, odd_swapped = real_form(2 * k), real_form(2 * k + 1), real_form(2 * swapped + 1)
    return np.stack([split(m) for m in (even, odd, odd.T, odd_swapped)])


EVEN, ODD_SWAPPED, EVEN_T, ODD_SWAPPED_T, EVEN_T_PIECES, ODD_T_PIECES, ODD = range(7)


def place_tables(shipped, full):
    window = full.shape[2]
    half = window // 2
    quarter = half // 2
    for level in range(2):
        even, odd, odd_t, swapped = (shipped[number, level] for number in range(4))
        full[EVEN, level] = even
        full[ODD, level] = odd
        full[ODD_SWAPPED, level] = swapped
        even_t = jnp.concatenate([
            jnp.concatenate([even[:half, :half], even[half:, :half]], axis=1),
            jnp.concatenate([even[:half, half:], even[half:, half:]], axis=1)], axis=0)
        full[EVEN_T, level] = even_t
        for block in range(4):
            to = (block ^ 1) * quarter
            full[ODD_SWAPPED_T, level, to:to + quarter, :] = (
                odd_t[block * quarter:(block + 1) * quarter])
        for first in range(0, half, PIECE):
            for part in range(2):
                to = slice(2 * first + part * PIECE, 2 * first + (part + 1) * PIECE)
                of = slice(part * half + first, part * half + first + PIECE)
                full[EVEN_T_PIECES, level, to, :] = even_t[of]
                full[ODD_T_PIECES, level, to, :] = odd_t[of]


def split_high_low(x):
    high = x.astype(jnp.bfloat16)
    low = (x - high.astype(jnp.float32)).astype(jnp.bfloat16)
    return high, low


def copies(pairs, sems):
    started = []
    for number, (source, target) in enumerate(pairs):
        copy = pltpu.make_async_copy(source, target, sems.at[number])
        copy.start()
        started.append(copy)
    return started


def process_slots(
    first_part, early, plan_ref, scale_ref, probe_ref, tables_ref, amplitudes, extended, total,
    stages,
):
    window = probe_ref.shape[1]
    half = window // 2
    places = amplitudes.shape[0]

    pieces = []
    for first in range(0, half, PIECE):
        for at_half in range(2):
            begin = 2 * first + at_half * PIECE
            pieces.append((slice(begin, begin + PIECE),
                           slice(at_half * half + first, at_half * half + first + PIECE)))

    lane = lax.broadcasted_iota(jnp.int32, (PIECE, LANES), 1)
    to_even_first = jnp.where(lane < half // 2, 2 * lane, 2 * lane - half + 1)
    to_odd_first = jnp.where(lane < half // 2, 2 * lane + 1, 2 * lane - half)
    lower = lane < half // 2

    def tall(block):
        high, low = block[:window], block[window:]
        return jnp.concatenate([high, high, low], axis=0)

    def wide(sides):
        high, low = sides[:, :window], sides[:, window:]
        return jnp.concatenate([high, high, low], axis=1)

    def right(sides, number):
        high, low = tables_ref[number, 0], tables_ref[number, 1]
        return jnp.dot(wide(sides), jnp.concatenate([high, low, high], axis=0),
                       preferred_element_type=jnp.float32)

    def left(number, block):
        high, low = tables_ref[number, 0], tables_ref[number, 1]
        return jnp.dot(jnp.concatenate([high, low, high], axis=1), tall(block),
                       preferred_element_type=jnp.float32)

    def process(index, which):
        probe_rolled, wave, side_even, side_odd, block_u, block_v = (
            ref.at[which] for ref in stages)
        row = plan_ref[HEAD + places + 2 * index]
        column = plan_ref[HEAD + places + 2 * index + 1]
        tile = column // LANES
        offset = column - tile * LANES
        last_tile = jnp.minimum(tile + 2, extended.shape[1] - 1)
        at = pl.ds(row, window)
        moved = lax.broadcasted_iota(jnp.int32, (window, LANES), 1) < offset

        for part in range(2):
            first = pltpu.roll(probe_ref[part, :, :LANES], offset, 1)
            second = pltpu.roll(probe_ref[part, :, LANES:], offset, 1)
            probe_rolled[part, 0] = jnp.where(moved, second, first)
            probe_rolled[part, 1] = jnp.where(moved, first, second)
        for side in range(2):
            if side == 0:
                view = [
                    jnp.where(moved, extended[p, last_tile, at, :], extended[p, tile, at, :])
                    for p in range(2)
                ]
            else:
                view = [extended[p, tile + 1, at, :] for p in range(2)]
            p_re, p_im = probe_rolled[0, side], probe_rolled[1, side]
            wave[0, side] = p_re * view[0] - p_im * view[1]
            wave[1, side] = p_re * view[1] + p_im * view[0]
        yield
        for number, sides in ((0, side_even), (1, side_odd)):
            for part in range(2):
                x = wave[part, 0] + wave[part, 1] if number == 0 else wave[part, 0] - wave[part, 1]
                high, low = split_high_low(x)
                lanes = slice(part * LANES, (part + 1) * LANES)
                for to, of in pieces:
                    sides[to, lanes] = high[of]
                    sides[to, window + part * LANES:window + (part + 1) * LANES] = low[of]
            y = right(sides, EVEN if number == 0 else ODD_SWAPPED)
            yield
            to = slice(number * LANES, (number + 1) * LANES)
            for first in range(0, half, PIECE):
                upper = y[2 * first:2 * first + PIECE]
                under = y[2 * first + PIECE:2 * first + 2 * PIECE]
                for block, x in ((block_u, upper + under), (block_v, upper - under)):
                    high, low = split_high_low(x)
                    for part in range(2):
                        lanes = slice(part * LANES, (part + 1) * LANES)
                        row_at = part * half + first
                        block[row_at:row_at + PIECE, to] = high[:, lanes]
                        block[window + row_at:window + row_at + PIECE, to] = low[:, lanes]

            yield
        for number, block in ((0, block_u), (1, block_v)):
            z = left(EVEN_T_PIECES if number == 0 else ODD_T_PIECES, block)
            yield
            for first in range(0, half, PIECE):
                z_re = z[2 * first:2 * first + PIECE]
                z_im = z[2 * first + PIECE:2 * first + 2 * PIECE]
                picked = [
                    amplitudes[index, t, pl.ds(number + 2 * first, PIECE, stride=2), :]
                    for t in range(2)
                ]
                g0 = jnp.take_along_axis(picked[0], to_even_first, axis=1)
                g1 = jnp.take_along_axis(picked[1], to_odd_first, axis=1)
                for t, amplitude in ((0, jnp.where(lower, g0, g1)), (1, jnp.where(lower, g1, g0))):
                    lanes = slice(t * LANES, (t + 1) * LANES)
                    a, b = z_re[:, lanes], z_im[:, lanes]
                    power = jnp.maximum(a * a + b * b, FLOOR_VALUE * FLOOR_VALUE)
                    ratio = amplitude * lax.rsqrt(power)
                    for part, x in ((0, a * ratio), (1, b * ratio)):
                        high, low = split_high_low(x)
                        row_at = part * half + first
                        block[row_at:row_at + PIECE, lanes] = high
                        block[window + row_at:window + row_at + PIECE, lanes] = low
            yield
        p, q = left(EVEN, block_u), left(ODD, block_v)
        yield
        for rows_half, x in ((0, p + q), (1, p - q)):
            high, low = split_high_low(x)
            to = slice(rows_half * half, (rows_half + 1) * half)
            for number, sides in ((0, side_even), (1, side_odd)):
                lanes = slice(number * LANES, (number + 1) * LANES)
                for part in range(2):
                    of = slice(part * half, (part + 1) * half)
                    sides[to, part * LANES:(part + 1) * LANES] = high[of, lanes]
                    sides[to, window + part * LANES:window + (part + 1) * LANES] = low[of, lanes]
        yield
        p, q = right(side_even, EVEN_T), right(side_odd, ODD_SWAPPED_T)
        yield
        scale = scale_ref[:1]
        for side, x in ((0, p + q), (1, p - q)):
            d_re = (x[:, :LANES] - wave[0, side]) * scale
            d_im = (x[:, LANES:] - wave[1, side]) * scale
            p_re, p_im = probe_rolled[0, side], probe_rolled[1, side]
            g = (p_re * d_re + p_im * d_im, p_re * d_im - p_im * d_re)
            for part in range(2):
                if side == 0:
                    total[part, tile, at, :] += jnp.where(moved, 0.0, g[part])
                    total[part, last_tile, at, :] += jnp.where(moved, g[part], 0.0)
                else:
                    total[part, tile + 1, at, :] += g[part]

    split = jnp.minimum(plan_ref[0], early)
    begin, end = (0, split) if first_part else (split, plan_ref[1])
    count = end - begin

    def two(pair, carry):
        first = process(plan_ref[HEAD + begin + 2 * pair], 0)
        second = process(plan_ref[HEAD + begin + 2 * pair + 1], 1)
        next(first)
        for _ in second:
            next(first, None)
        return carry

    lax.fori_loop(0, count // 2, two, 0)

    @pl.when(count % 2 == 1)
    def _():
        for _ in process(plan_ref[HEAD + end - 1], 0):
            pass


def corners_kernel(center, near, far, sems):
    height, width = center.shape[1:]
    pairs = []
    for which, ref in ((NEAR, near), (FAR, far)):
        row = pl.multiple_of(is_after("narrow", which) * (height - HALO), HALO)
        for part in range(2):
            for to, lane in ((0, 0), (HALO, width - HALO)):
                pairs.append((center.at[part, pl.ds(row, HALO), pl.ds(lane, HALO)],
                              ref.at[part, :, pl.ds(to, HALO)]))
    for copy in copies(pairs, sems):
        copy.wait()


def edges_kernel(center, near_columns, far_columns, near_rows, far_rows, sems):
    height, width = center.shape[1:]
    pairs = []
    for which, columns, rows in ((NEAR, near_columns, near_rows), (FAR, far_columns, far_rows)):
        row = pl.multiple_of(is_after("narrow", which) * (height - HALO), HALO)
        lane = pl.multiple_of(is_after("wide", which) * (width - HALO), HALO)
        for part in range(2):
            pairs += [
                (center.at[part, :, pl.ds(lane, HALO)], columns.at[part]),
                (center.at[part, pl.ds(row, HALO), pl.ds(HALO, width - 2 * HALO)], rows.at[part]),
            ]
    for copy in copies(pairs, sems):
        copy.wait()


def setup_kernel(
    starts_in, live_in, center, measured_ref, probe_in, tables_in, extended, total, amplitudes,
    scale, probe, tables_full, plan, tables_got, starts_ref, live_ref, sems, amplitude_sems,
):
    own = pl.ds(HALO, center.shape[1])
    tiles = extended.shape[1]
    subsets, slots = measured_ref.shape[2:4]
    *small, = copies([(starts_in, starts_ref), (live_in, live_ref)], sems)
    started = copies(
        [(probe_in, probe), (tables_in, tables_got)]
        + [(center.at[part, :, pl.ds(tile * LANES, LANES)], extended.at[part, tile + 1, own, :])
           for part in range(2) for tile in range(tiles - 2)],
        sems.at[pl.ds(2, sems.shape[0] - 2)])
    for copy in small:
        copy.wait()

    def each_live(act):
        def one(number, carry):
            subset = number // slots
            slot = number - subset * slots

            @pl.when(slot < live_ref[0, 0, subset])
            def _():
                for tile in range(2):
                    act(pltpu.make_async_copy(
                        measured_ref.at[0, 0, subset, slot, :, pl.ds(tile * LANES, LANES)],
                        amplitudes.at[number, tile], amplitude_sems.at[number, tile]))

            return carry

        lax.fori_loop(0, subsets * slots, one, 0)

    each_live(lambda copy: copy.start())

    places = subsets * slots
    window = amplitudes.shape[2]
    last_inner = center.shape[1] + HALO - window

    def sort(inner, number, count):
        subset = number // slots
        slot = number - subset * slots
        row = starts_ref[0, 0, subset, 0, slot]
        inside = (row >= HALO) & (row <= last_inner)
        mine = (slot < live_ref[0, 0, subset]) & (inside == inner)

        @pl.when(mine)
        def _():
            plan[HEAD + count] = number

        if inner:
            for axis in range(2):
                plan[HEAD + places + 2 * number + axis] = starts_ref[0, 0, subset, axis, slot]
        return count + mine.astype(jnp.int32)

    inner_count = lax.fori_loop(0, places, functools.partial(sort, True), jnp.int32(0))
    plan[0] = inner_count
    plan[1] = lax.fori_loop(0, places, functools.partial(sort, False), inner_count)
    total[...] = jnp.zeros_like(total)
    started[0].wait()
    squared = probe[0] * probe[0] + probe[1] * probe[1]
    scale[...] = jnp.broadcast_to(1.0 / jnp.max(squared, keepdims=True), scale.shape)
    started[1].wait()
    place_tables(tables_got, tables_full)
    for copy in started[2:]:
        copy.wait()
    each_live(lambda copy: copy.wait())


def slots_kernel(
    n_in, n_out, first_part, early, parts, outputs, plan_ref, scale_ref, probe_ref, tables_ref,
    amplitudes, *refs,
):
    arrived, refs = refs[:n_in], refs[n_in + 2:]
    extended, total, *refs = refs
    outs, scratch = refs[:n_out], refs[n_out:]

    def place(key, end):
        return key if isinstance(key, int) else is_after(*key) * end

    def pieces(entries, arrays):
        for number, of, row, rows, tiles in entries:
            if not isinstance(row, int):
                row = pl.multiple_of(place(row, extended.shape[2] - HALO), HALO)
            for part in range(2):
                for lane, tile in enumerate(tiles):
                    yield (arrays[number],
                           (part, slice(of, of + rows), slice(lane * LANES, (lane + 1) * LANES)),
                           (part, place(tile, extended.shape[1] - 1), pl.ds(row, rows)))

    for ref, here, there in pieces(parts, arrived):
        extended[there] = ref[here]
    process_slots(first_part, early, plan_ref, scale_ref, probe_ref, tables_ref, amplitudes,
                  extended, total, scratch)
    for ref, here, there in pieces(outputs, outs):
        ref[here] = total[there]


SMEM = pl.BlockSpec(memory_space=pltpu.SMEM)
VMEM = pl.BlockSpec(memory_space=pltpu.VMEM)
ANY = pl.BlockSpec(memory_space=pl.ANY)
HBM = pl.BlockSpec(memory_space=pltpu.HBM)
MIB = 1024 * 1024


def run_slots(first_part, early, common, extended, total, arrived, parts, outputs, out_shapes):
    window = common[2].shape[1]
    f32, bf16 = jnp.float32, jnp.bfloat16
    n = len(common) + len(arrived)
    return pl.pallas_call(
        functools.partial(slots_kernel, len(arrived), len(out_shapes), first_part, early, parts,
                          outputs),
        out_shape=[pltpu.VMEM(shape, f32)
                   for shape in [extended.shape, total.shape] + out_shapes],
        in_specs=[SMEM] + [VMEM] * (n + 1),
        out_specs=[VMEM] * (2 + len(out_shapes)),
        input_output_aliases={n: 0, n + 1: 1},
        scratch_shapes=[
            pltpu.VMEM((2, 2, 2, window, LANES), f32),
            pltpu.VMEM((2, 2, 2, window, LANES), f32),
            pltpu.VMEM((2, window, 2 * window), bf16),
            pltpu.VMEM((2, window, 2 * window), bf16),
            pltpu.VMEM((2, 2 * window, window), bf16),
            pltpu.VMEM((2, 2 * window, window), bf16),
        ],
        compiler_params=pltpu.CompilerParams(vmem_limit_bytes=12 * MIB),
        cost_estimate=pl.CostEstimate(
            flops=4 * 24 * 2 * window ** 3, bytes_accessed=12 * MIB, transcendentals=0),
    )(*common, *arrived, extended, total)


def sides(axis, near, far):
    near_after = is_after(axis, NEAR) == 1
    return jnp.where(near_after, far, near), jnp.where(near_after, near, far)


def ends_kernel(near_outer, far_outer, near, far):
    for which, ref in ((NEAR, near), (FAR, far)):
        after = is_after("wide", which) == 1
        for number, rim in enumerate((near_outer, far_outer)):
            ref[:, number * HALO:(number + 1) * HALO, :] = jnp.where(
                after, rim[:, :, HALO:], rim[:, :, :HALO])


def folded_kernel(near_ends, far_ends, near_rim, far_rim, near, far):
    left, right = sides("wide", near_rim[...], far_rim[...])
    for number, (ref, ends) in enumerate(((near, near_ends), (far, far_ends))):
        rows = slice(number * HALO, (number + 1) * HALO)
        ref[:, :, :HALO] = ends[:, :, :HALO] + left[:, rows]
        ref[:, :, HALO:] = ends[:, :, HALO:] + right[:, rows]


def tail_kernel(
    extended, total, near_side, far_side, near_middle, far_middle, out, head, foot, kept, sems,
):
    height, width = kept.shape[1:]
    own = slice(HALO, HALO + height)
    for part in range(2):
        for tile in range(width // LANES):
            kept[part, :, tile * LANES:(tile + 1) * LANES] = (
                extended[part, tile + 1, own, :] + total[part, tile + 1, own, :])
        left, right = sides("wide", near_side[part], far_side[part])
        kept[part, :, :HALO] += left
        kept[part, :, width - HALO:] += right
        above, below = sides("narrow", near_middle[part], far_middle[part])
        kept[part, :HALO, HALO:width - HALO] += above
        kept[part, height - HALO:, HALO:width - HALO] += below
    rows = pl.ds(HALO, height - 2 * HALO)
    started = copies([(kept.at[part, rows, :], out.at[part, rows, :]) for part in range(2)], sems)
    head[...] = kept[:, :HALO, :]
    foot[...] = kept[:, height - HALO:, :]
    for copy in started:
        copy.wait()


def rims_kernel(head, foot, near_outer, far_outer, old, out, head_kept, foot_kept, sems):
    height, width = out.shape[1:]
    started = []
    outer = sides("narrow", near_outer[...], far_outer[...])
    for number, (ref, kept, row) in enumerate((
        (head, head_kept, 0), (foot, foot_kept, height - HALO),
    )):
        kept[...] = ref[...]
        kept[:, :, :HALO] += outer[number][:, :, :HALO]
        kept[:, :, width - HALO:] += outer[number][:, :, HALO:]
        started += copies(
            [(kept.at[part], out.at[part, pl.ds(row, HALO), :]) for part in range(2)],
            sems.at[pl.ds(2 * number, 2)])
    for copy in started:
        copy.wait()


def update(transmission, probe_wave, positions, counts, measured):
    height, width = transmission.shape[1:]
    window = probe_wave.shape[1]
    slots = measured.shape[3]
    tiles = (width + 2 * HALO) // LANES
    whole = (2, tiles, height + 2 * HALO, LANES)
    wide_rim, side = (2, HALO, width), (2, height, HALO)
    outer, middle = (2, HALO, 2 * HALO), (2, HALO, width - 2 * HALO)
    f32 = jnp.float32
    transmission = pltpu.with_memory_space_constraint(transmission, pltpu.HBM)
    near_outer, far_outer = pl.pallas_call(
        corners_kernel, name="corners",
        out_shape=[pltpu.VMEM(outer, f32)] * 2,
        in_specs=[HBM], out_specs=[VMEM] * 2,
        scratch_shapes=[pltpu.SemaphoreType.DMA((8,))],
        compiler_params=pltpu.CompilerParams(vmem_limit_bytes=4 * MIB),
    )(transmission)

    def exchange(axis, near, far):
        from_far = swapped(far, axis, FAR)
        return swapped(near, axis, NEAR), from_far

    near_outer, far_outer = exchange("narrow", near_outer, far_outer)
    near_columns, far_columns, near_middle, far_middle = pl.pallas_call(
        edges_kernel, name="edges",
        out_shape=[pltpu.VMEM(shape, f32) for shape in (side, side, middle, middle)],
        in_specs=[HBM], out_specs=[VMEM] * 4,
        scratch_shapes=[pltpu.SemaphoreType.DMA((8,))],
        compiler_params=pltpu.CompilerParams(vmem_limit_bytes=4 * MIB),
    )(transmission)
    near_columns, far_columns = exchange("wide", near_columns, far_columns)

    table = jnp.asarray(tables(window))
    extended, total, amplitudes, scale, probe, full, plan = pl.pallas_call(
        setup_kernel, name="setup",
        out_shape=[
            pltpu.VMEM(whole, f32), pltpu.VMEM(whole, f32),
            pltpu.VMEM((2 * slots, 2, window, LANES), f32), pltpu.VMEM((8, LANES), f32),
            pltpu.VMEM(probe_wave.shape, f32),
            pltpu.VMEM((7, *table.shape[1:]), table.dtype),
            jax.ShapeDtypeStruct((HEAD + 6 * slots,), jnp.int32)],
        in_specs=[HBM] * 6, out_specs=[VMEM] * 6 + [SMEM],
        scratch_shapes=[
            pltpu.VMEM(table.shape, table.dtype),
            pltpu.SMEM((1, 1, 2, 2, slots), jnp.int32), pltpu.SMEM(counts.shape, jnp.int32),
            pltpu.SemaphoreType.DMA((4 + 2 * (tiles - 2),)),
            pltpu.SemaphoreType.DMA((2 * slots, 2))],
        compiler_params=pltpu.CompilerParams(vmem_limit_bytes=12 * MIB),
        cost_estimate=pl.CostEstimate(
            flops=0, bytes_accessed=8 * MIB, transcendentals=0),
    )(*(pltpu.with_memory_space_constraint(x, pltpu.HBM)
        for x in (jnp.swapaxes(positions, 3, 4), counts, transmission, measured, probe_wave,
                  table)))
    common = (plan, scale, probe, full, amplitudes)
    near_middle, far_middle = exchange("narrow", near_middle, far_middle)

    def small_kernel(kernel, outs, *ins):
        return pl.pallas_call(
            kernel,
            out_shape=[pltpu.VMEM(shape, f32) for shape in outs],
            in_specs=[VMEM] * len(ins), out_specs=[VMEM] * len(outs),
            compiler_params=pltpu.CompilerParams(vmem_limit_bytes=4 * MIB),
        )(*ins)

    both = (2, 2 * HALO, HALO)
    near_corner, far_corner = exchange(
        "wide", *small_kernel(ends_kernel, [both] * 2, near_outer, far_outer))

    inner_tiles, ends = tuple(range(2, tiles - 2)), (1, tiles - 2)
    beside = (("wide", NEAR),), (("wide", FAR),)
    near_row, far_row = ("narrow", NEAR), ("narrow", FAR)
    extended, total = run_slots(
        True, EARLY, common, extended, total,
        (near_columns, far_columns),
        ((NEAR, 0, HALO, height, beside[NEAR]), (FAR, 0, HALO, height, beside[FAR])), (), [])
    rows_in = (
        (0, 0, near_row, HALO, inner_tiles), (1, 0, far_row, HALO, inner_tiles),
        (2, 0, near_row, HALO, ends), (3, 0, far_row, HALO, ends),
        *((4 + which, of, row, HALO, beside[which])
          for which in (NEAR, FAR) for of, row in ((0, near_row), (HALO, far_row))))
    (extended, total, near_up, far_up, near_ends, far_ends, near_rim, far_rim, near_side,
     far_side) = run_slots(
        False, EARLY, common, extended, total,
        (near_middle, far_middle, near_outer, far_outer, near_corner, far_corner), rows_in,
        rows_in + ((6, 0, HALO, height, beside[NEAR]), (7, 0, HALO, height, beside[FAR])),
        [middle, middle, outer, outer, both, both, side, side])
    near_up, far_up = exchange("narrow", near_up, far_up)
    near_rim, far_rim = exchange("wide", near_rim, far_rim)

    near_ends, far_ends = exchange(
        "narrow", *small_kernel(
            folded_kernel, [outer] * 2, near_ends, far_ends, near_rim, far_rim))
    near_side, far_side = exchange("wide", near_side, far_side)

    out, head, foot = pl.pallas_call(
        tail_kernel, name="tail",
        out_shape=[jax.ShapeDtypeStruct((2, height, width), f32),
                   pltpu.VMEM(wide_rim, f32), pltpu.VMEM(wide_rim, f32)],
        in_specs=[VMEM] * 6, out_specs=[ANY, VMEM, VMEM],
        scratch_shapes=[pltpu.VMEM((2, height, width), f32), pltpu.SemaphoreType.DMA((2,))],
        compiler_params=pltpu.CompilerParams(vmem_limit_bytes=8 * MIB),
    )(extended, total, near_side, far_side, near_up, far_up)
    return pl.pallas_call(
        rims_kernel, name="rims",
        out_shape=jax.ShapeDtypeStruct((2, height, width), f32),
        in_specs=[VMEM] * 4 + [ANY], out_specs=ANY,
        input_output_aliases={4: 0},
        scratch_shapes=[pltpu.VMEM(wide_rim, f32), pltpu.VMEM(wide_rim, f32),
                        pltpu.SemaphoreType.DMA((4,))],
        compiler_params=pltpu.CompilerParams(vmem_limit_bytes=4 * MIB),
    )(head, foot, near_ends, far_ends, out)


def solution(mesh):
    in_specs = (
        P(None, "narrow", "wide"),
        P(),
        P("narrow", "wide", None, None, None),
        P("narrow", "wide", None),
        P("narrow", "wide", None, None, None, None),
    )
    out_specs = P(None, "narrow", "wide")
    return jax.shard_map(update, mesh=mesh, in_specs=in_specs, out_specs=out_specs, check_vma=False)
```

time: 99.6 us -> 74.1 us (0.74)
  the two profiles are of different devices: /device:TPU:25 before, /device:TPU:28 now
where the time goes in v2:
time: 74.1 us; the launch traced here: 73.7 us
  waiting for transfers between devices  30.2 us (41%)
  Pallas kernels  22.5 us (30%)
  starting transfers between devices  20.8 us (28%)
    ppermute x16, waiting for transfers between devices, swapped(): return lax.ppermute(shard, axis, pairs)  30.2 us
    ppermute x16, starting transfers between devices, swapped(): return lax.ppermute(shard, axis, pairs)  20.8 us
    pallas_call x2, Pallas kernels, run_slots(): pl.pallas_call(functools.partial(slots_kernel, len(arrived), len(out_shap...  13.3 us
    pallas_call x1, Pallas kernels, update(): pl.pallas_call(setup_kernel, name='setup', out_shape=[pltpu.VMEM(whole, f...  3.75 us
    pallas_call x1, Pallas kernels, update(): pl.pallas_call(tail_kernel, name='tail', out_shape=[jax.ShapeDtypeStruct(...  1.64 us
  transfers between devices with their start and end apart: 16, of which 4 were waited for; matrix products, arithmetic and copies ran while one was open for 0% of the time, Pallas kernels for 16%

profile of v2, /device:TPU:28, one launch (start us, length us, event | category | flops | bytes accessed | tf_op | source)
XLA Modules:
  0.0 73.7 jit_solution(4476321498172321227)
XLA Ops:
  0.0 1.4 %edges.1 = (f32[2,512,128]{2,1,0:T(8,128)S(1)}, f32[2,512,128]{2,1,0:T(8,128)S(1)}, f32[2,128,256]{2,1,0:T(8,128)S(1)}, f32[2,128,256]{2,1,0:T(8,128)S(1)}) custom-call(f32[2,512,512]{2,1,0:T(8,128)} %center.5), custom_call_target="tpu_custom_call" | custom-call | tf_op jit(solution)/shard_map/edges/pallas_call | solution.py:498
  1.5 0.1 collective-permute-start.6
  1.5 2.5 %collective-permute-start.7 = (f32[2,512,128]{2,1,0:T(8,128)S(1)}, f32[2,512,128]{2,1,0:T(8,128)S(1)}, u32[]{:S(2)}, u32[]{:S(2)}) collective-permute-start(f32[2,512,128]{2,1,0:T(8,128)S(1)} %get-tuple-element.49), channel_id=1, source_target_pairs={{8,16},{16,8},{9,17},{17,9},{10,18},{18,10},{11,19},{19,11},{12,20... | collective-permute-start | bytes 1572872 | tf_op jit(solution)/shard_map/ppermute | solution.py:25
  4.0 1.1 %corners.1 = (f32[2,128,256]{2,1,0:T(8,128)S(1)}, f32[2,128,256]{2,1,0:T(8,128)S(1)}) custom-call(f32[2,512,512]{2,1,0:T(8,128)} %center.5), custom_call_target="tpu_custom_call" | custom-call | tf_op jit(solution)/shard_map/corners/pallas_call | solution.py:485
  5.2 1.6 %collective-permute-start.2 = (f32[2,128,256]{2,1,0:T(8,128)S(1)}, f32[2,128,256]{2,1,0:T(8,128)S(1)}, u32[]{:S(2)}, u32[]{:S(2)}) collective-permute-start(f32[2,128,256]{2,1,0:T(8,128)S(1)} %get-tuple-element.44), channel_id=1, source_target_pairs={{0,1},{1,0},{2,3},{3,2},{4,5},{5,4},{6,7},{7,6},{8,9},{9,8},{10,11... | collective-permute-start | bytes 786440 | tf_op jit(solution)/shard_map/ppermute | solution.py:25
  6.8 2.3 %collective-permute-start.3 = (f32[2,128,256]{2,1,0:T(8,128)S(1)}, f32[2,128,256]{2,1,0:T(8,128)S(1)}, u32[]{:S(2)}, u32[]{:S(2)}) collective-permute-start(f32[2,128,256]{2,1,0:T(8,128)S(1)} %get-tuple-element.45), channel_id=1, source_target_pairs={{1,2},{2,1},{3,4},{4,3},{5,6},{6,5},{9,10},{10,9},{11,12},{12,11},... | collective-permute-start | bytes 786440 | tf_op jit(solution)/shard_map/ppermute | solution.py:25
  9.1 0.1 collective-permute-start
  9.2 3.8 %setup.1 = (f32[2,6,768,128]{3,2,1,0:T(8,128)S(1)}, f32[2,6,768,128]{3,2,1,0:T(8,128)S(1)}, f32[12,2,256,128]{3,2,1,0:T(8,128)S(1)}, f32[8,128]{1,0:T(8,128)S(1)...) custom-call(s32[1,1,2,2,6]{4,3,2,1,0:T(2,128)} %bitcast.1, s32[1,1,2]{2,1,0:T(1,128)} %live_in.1, ...), custom_call_target="tpu_custom_call" | custom-call | bytes 8388608 | tf_op jit(solution)/shard_map/setup/pallas_call | solution.py:508
  12.9 10.0 %collective-permute-done.2.near_outer.refs_2_ = f32[2,128,256]{2,1,0:T(8,128)S(1)} collective-permute-done((f32[2,128,256]{2,1,0:T(8,128)S(1)}, f32[2,128,256]{2,1,0:T(8,128)S(1)}, u32[]{:S(2)}, u32[]{:S(2)}) %collective-permute-start.2) | collective-permute-done | bytes 262176 | tf_op jit(solution)/shard_map/ppermute | solution.py:25
  22.9 1.9 %collective-permute-start.1 = (f32[2,128,256]{2,1,0:T(8,128)S(1)}, f32[2,128,256]{2,1,0:T(8,128)S(1)}, u32[]{:S(2)}, u32[]{:S(2)}) collective-permute-start(f32[2,128,256]{2,1,0:T(8,128)S(1)} %get-tuple-element.43), channel_id=1, source_target_pairs={{1,2},{2,1},{3,4},{4,3},{5,6},{6,5},{9,10},{10,9},{11,12},{12,11},... | collective-permute-start | bytes 786440 | tf_op jit(solution)/shard_map/ppermute | solution.py:25
  25.0 1.9 %collective-permute-start.5 = (f32[2,256,128]{2,1,0:T(8,128)S(1)}, f32[2,256,128]{2,1,0:T(8,128)S(1)}, u32[]{:S(2)}, u32[]{:S(2)}) collective-permute-start(f32[2,256,128]{2,1,0:T(8,128)S(1)} %get-tuple-element.47), channel_id=1, source_target_pairs={{8,16},{16,8},{9,17},{17,9},{10,18},{18,10},{11,19},{19,11},{12,20... | collective-permute-start | bytes 786440 | tf_op jit(solution)/shard_map/ppermute | solution.py:25
  26.9 5.2 %shard_map.65 = (f32[2,6,768,128]{3,2,1,0:T(8,128)S(1)}, f32[2,6,768,128]{3,2,1,0:T(8,128)S(1)}) custom-call(s32[38]{0:T(128)S(1)} %get-tuple-element.37.plan_ref, f32[8,128]{1,0:T(8,128)S(1)} %get-tuple-element.38.scale_ref, f32[2,256,256]{2,1,0:T(8,128)S(1)} %get-tuple-element.39.probe_ref, ...), custom_call_target="tpu_custom_call", output_to_operand_aliasing={{0}: (7, {}), {1}: (8, {})} | custom-call | flops 3221225472 | bytes 12582912 | tf_op jit(solution)/shard_map/pallas_call | solution.py:392
  32.2 0.5 collective-permute-done.5.refs_5_
  32.7 8.1 %shard_map.66 = (f32[2,6,768,128]{3,2,1,0:T(8,128)S(1)}, f32[2,6,768,128]{3,2,1,0:T(8,128)S(1)}, f32[2,128,256]{2,1,0:T(8,128)S(1)}, f32[2,128,256]{2,1,0:T(8,12...) custom-call(s32[38]{0:T(128)S(1)} %get-tuple-element.37.plan_ref, ...), custom_call_target="tpu_custom_call", output_to_operand_aliasing={{0}: (11, {}), {1}: (12, {})} | custom-call | flops 3221225472 | bytes 12582912 | tf_op jit(solution)/shard_map/pallas_call | solution.py:392
  40.8 1.9 %collective-permute-start.13 = (f32[2,256,128]{2,1,0:T(8,128)S(1)}, f32[2,256,128]{2,1,0:T(8,128)S(1)}, u32[]{:S(2)}, u32[]{:S(2)}) collective-permute-start(f32[2,256,128]{2,1,0:T(8,128)S(1)} %get-tuple-element.65), channel_id=1, source_target_pairs={{8,16},{16,8},{9,17},{17,9},{10,18},{18,10},{11,19},{19,11},{12,20... | collective-permute-start | bytes 786440 | tf_op jit(solution)/shard_map/ppermute | solution.py:25
  42.8 3.6 %collective-permute-start.9 = (f32[2,512,128]{2,1,0:T(8,128)S(1)}, f32[2,512,128]{2,1,0:T(8,128)S(1)}, u32[]{:S(2)}, u32[]{:S(2)}) collective-permute-start(f32[2,512,128]{2,1,0:T(8,128)S(1)} %get-tuple-element.57), channel_id=1, source_target_pairs={{8,16},{16,8},{9,17},{17,9},{10,18},{18,10},{11,19},{19,11},{12,20... | collective-permute-start | bytes 1572872 | tf_op jit(solution)/shard_map/ppermute | solution.py:25
  46.6 1.9 %collective-permute-start.11 = (f32[2,128,256]{2,1,0:T(8,128)S(1)}, f32[2,128,256]{2,1,0:T(8,128)S(1)}, u32[]{:S(2)}, u32[]{:S(2)}) collective-permute-start(f32[2,128,256]{2,1,0:T(8,128)S(1)} %get-tuple-element.59), channel_id=1, source_target_pairs={{1,2},{2,1},{3,4},{4,3},{5,6},{6,5},{9,10},{10,9},{11,12},{12,11},... | collective-permute-start | bytes 786440 | tf_op jit(solution)/shard_map/ppermute | solution.py:25
  48.5 0.1 shard_map.67
  48.6 0.8 %collective-permute-start.14 = (f32[2,128,256]{2,1,0:T(8,128)S(1)}, f32[2,128,256]{2,1,0:T(8,128)S(1)}, u32[]{:S(2)}, u32[]{:S(2)}) collective-permute-start(f32[2,128,256]{2,1,0:T(8,128)S(1)} %get-tuple-element.66), channel_id=1, source_target_pairs={{0,1},{1,0},{2,3},{3,2},{4,5},{5,4},{6,7},{7,6},{8,9},{9,8},{10,11... | collective-permute-start | bytes 786440 | tf_op jit(solution)/shard_map/ppermute | solution.py:25
  49.4 14.1 %collective-permute-done.10.near_middle = f32[2,128,256]{2,1,0:T(8,128)S(1)} collective-permute-done((f32[2,128,256]{2,1,0:T(8,128)S(1)}, f32[2,128,256]{2,1,0:T(8,128)S(1)}, u32[]{:S(2)}, u32[]{:S(2)}) %collective-permute-start.10) | collective-permute-done | bytes 262176 | tf_op jit(solution)/shard_map/ppermute | solution.py:25
  63.5 1.9 %collective-permute-start.15 = (f32[2,128,256]{2,1,0:T(8,128)S(1)}, f32[2,128,256]{2,1,0:T(8,128)S(1)}, u32[]{:S(2)}, u32[]{:S(2)}) collective-permute-start(f32[2,128,256]{2,1,0:T(8,128)S(1)} %get-tuple-element.67), channel_id=1, source_target_pairs={{1,2},{2,1},{3,4},{4,3},{5,6},{6,5},{9,10},{10,9},{11,12},{12,11},... | collective-permute-start | bytes 786440 | tf_op jit(solution)/shard_map/ppermute | solution.py:25
  65.5 1.6 %tail.1 = (f32[2,512,512]{2,1,0:T(8,128)}, f32[2,128,512]{2,1,0:T(8,128)S(1)}, f32[2,128,512]{2,1,0:T(8,128)S(1)}) custom-call(f32[2,6,768,128]{3,2,1,0:T(8,128)S(1)} %get-tuple-element.54.extended, f32[2,6,768,128]{3,2,1,0:T(8,128)S(1)} %get-tuple-element.55.total, f32[2,512,128]{2,1,0:T(8,128)S(1)} %collective-permute-done.8.near_side, ...), custom_call_target="tpu_custom_call" | custom-call | tf_op jit(solution)/shard_map/tail/pallas_call | solution.py:569
  67.1 5.5 %collective-permute-done.15.far_outer = f32[2,128,256]{2,1,0:T(8,128)S(1)} collective-permute-done((f32[2,128,256]{2,1,0:T(8,128)S(1)}, f32[2,128,256]{2,1,0:T(8,128)S(1)}, u32[]{:S(2)}, u32[]{:S(2)}) %collective-permute-start.15) | collective-permute-done | bytes 262176 | tf_op jit(solution)/shard_map/ppermute | solution.py:25
  72.7 1.1 %rims.1 = f32[2,512,512]{2,1,0:T(8,128)} custom-call(f32[2,128,512]{2,1,0:T(8,128)S(1)} %get-tuple-element.60.head, f32[2,128,512]{2,1,0:T(8,128)S(1)} %get-tuple-element.61.foot, f32[2,128,256]{2,1,0:T(8,128)S(1)} %collective-permute-done.14.near_outer, f32[2,128,256]{2,1,0:T(8,128)S(1)} %collective-permute-done.15.far_outer, ...), custom_call_target="tpu_custom_call", output_to_operand_aliasing={{}: (4, {})} | custom-call | tf_op jit(solution)/shard_map/rims/pallas_call | solution.py:577
  (17 shorter events, 0.4 us)
Async XLA Ops:
  1.5 23.5 %collective-permute-start.6 = (f32[2,512,128]{2,1,0:T(8,128)S(1)}, f32[2,512,128]{2,1,0:T(8,128)S(1)}, u32[]{:S(2)}, u32[]{:S(2)}) collective-permute-start(f32[2,512,128]{2,1,0:T(8,128)S(1)} %get-tuple-element.48), channel_id=1, source_target_pairs={{0,8},{8,0},{16,24},{24,16},{1,9},{9,1},{17,25},{25,17},{2,10},{10... | collective-permute-start | bytes 1572872 | tf_op jit(solution)/shard_map/ppermute | solution.py:25
  1.5 25.4 %collective-permute-start.7 = (f32[2,512,128]{2,1,0:T(8,128)S(1)}, f32[2,512,128]{2,1,0:T(8,128)S(1)}, u32[]{:S(2)}, u32[]{:S(2)}) collective-permute-start(f32[2,512,128]{2,1,0:T(8,128)S(1)} %get-tuple-element.49), channel_id=1, source_target_pairs={{8,16},{16,8},{9,17},{17,9},{10,18},{18,10},{11,19},{19,11},{12,20... | collective-permute-start | bytes 1572872 | tf_op jit(solution)/shard_map/ppermute | solution.py:25
  5.2 17.7 %collective-permute-start.2 = (f32[2,128,256]{2,1,0:T(8,128)S(1)}, f32[2,128,256]{2,1,0:T(8,128)S(1)}, u32[]{:S(2)}, u32[]{:S(2)}) collective-permute-start(f32[2,128,256]{2,1,0:T(8,128)S(1)} %get-tuple-element.44), channel_id=1, source_target_pairs={{0,1},{1,0},{2,3},{3,2},{4,5},{5,4},{6,7},{7,6},{8,9},{9,8},{10,11... | collective-permute-start | bytes 786440 | tf_op jit(solution)/shard_map/ppermute | solution.py:25
  6.8 18.0 %collective-permute-start.3 = (f32[2,128,256]{2,1,0:T(8,128)S(1)}, f32[2,128,256]{2,1,0:T(8,128)S(1)}, u32[]{:S(2)}, u32[]{:S(2)}) collective-permute-start(f32[2,128,256]{2,1,0:T(8,128)S(1)} %get-tuple-element.45), channel_id=1, source_target_pairs={{1,2},{2,1},{3,4},{4,3},{5,6},{6,5},{9,10},{10,9},{11,12},{12,11},... | collective-permute-start | bytes 786440 | tf_op jit(solution)/shard_map/ppermute | solution.py:25
  9.1 23.0 %collective-permute-start = (f32[2,128,256]{2,1,0:T(8,128)S(1)}, f32[2,128,256]{2,1,0:T(8,128)S(1)}, u32[]{:S(2)}, u32[]{:S(2)}) collective-permute-start(f32[2,128,256]{2,1,0:T(8,128)S(1)} %get-tuple-element.42), channel_id=1, source_target_pairs={{0,1},{1,0},{2,3},{3,2},{4,5},{5,4},{6,7},{7,6},{8,9},{9,8},{10,11... | collective-permute-start | bytes 786440 | tf_op jit(solution)/shard_map/ppermute | solution.py:25
  22.9 9.3 %collective-permute-start.1 = (f32[2,128,256]{2,1,0:T(8,128)S(1)}, f32[2,128,256]{2,1,0:T(8,128)S(1)}, u32[]{:S(2)}, u32[]{:S(2)}) collective-permute-start(f32[2,128,256]{2,1,0:T(8,128)S(1)} %get-tuple-element.43), channel_id=1, source_target_pairs={{1,2},{2,1},{3,4},{4,3},{5,6},{6,5},{9,10},{10,9},{11,12},{12,11},... | collective-permute-start | bytes 786440 | tf_op jit(solution)/shard_map/ppermute | solution.py:25
  24.9 7.3 %collective-permute-start.4 = (f32[2,256,128]{2,1,0:T(8,128)S(1)}, f32[2,256,128]{2,1,0:T(8,128)S(1)}, u32[]{:S(2)}, u32[]{:S(2)}) collective-permute-start(f32[2,256,128]{2,1,0:T(8,128)S(1)} %get-tuple-element.46), channel_id=1, source_target_pairs={{0,8},{8,0},{16,24},{24,16},{1,9},{9,1},{17,25},{25,17},{2,10},{10... | collective-permute-start | bytes 786440 | tf_op jit(solution)/shard_map/ppermute | solution.py:25
  25.0 7.7 %collective-permute-start.5 = (f32[2,256,128]{2,1,0:T(8,128)S(1)}, f32[2,256,128]{2,1,0:T(8,128)S(1)}, u32[]{:S(2)}, u32[]{:S(2)}) collective-permute-start(f32[2,256,128]{2,1,0:T(8,128)S(1)} %get-tuple-element.47), channel_id=1, source_target_pairs={{8,16},{16,8},{9,17},{17,9},{10,18},{18,10},{11,19},{19,11},{12,20... | collective-permute-start | bytes 786440 | tf_op jit(solution)/shard_map/ppermute | solution.py:25
  40.8 5.8 %collective-permute-start.12 = (f32[2,256,128]{2,1,0:T(8,128)S(1)}, f32[2,256,128]{2,1,0:T(8,128)S(1)}, u32[]{:S(2)}, u32[]{:S(2)}) collective-permute-start(f32[2,256,128]{2,1,0:T(8,128)S(1)} %get-tuple-element.64), channel_id=1, source_target_pairs={{0,8},{8,0},{16,24},{24,16},{1,9},{9,1},{17,25},{25,17},{2,10},{10... | collective-permute-start | bytes 786440 | tf_op jit(solution)/shard_map/ppermute | solution.py:25
  40.8 7.7 %collective-permute-start.13 = (f32[2,256,128]{2,1,0:T(8,128)S(1)}, f32[2,256,128]{2,1,0:T(8,128)S(1)}, u32[]{:S(2)}, u32[]{:S(2)}) collective-permute-start(f32[2,256,128]{2,1,0:T(8,128)S(1)} %get-tuple-element.65), channel_id=1, source_target_pairs={{8,16},{16,8},{9,17},{17,9},{10,18},{18,10},{11,19},{19,11},{12,20... | collective-permute-start | bytes 786440 | tf_op jit(solution)/shard_map/ppermute | solution.py:25
  42.8 22.7 %collective-permute-start.8 = (f32[2,512,128]{2,1,0:T(8,128)S(1)}, f32[2,512,128]{2,1,0:T(8,128)S(1)}, u32[]{:S(2)}, u32[]{:S(2)}) collective-permute-start(f32[2,512,128]{2,1,0:T(8,128)S(1)} %get-tuple-element.56), channel_id=1, source_target_pairs={{0,8},{8,0},{16,24},{24,16},{1,9},{9,1},{17,25},{25,17},{2,10},{10... | collective-permute-start | bytes 1572872 | tf_op jit(solution)/shard_map/ppermute | solution.py:25
  42.8 22.6 %collective-permute-start.9 = (f32[2,512,128]{2,1,0:T(8,128)S(1)}, f32[2,512,128]{2,1,0:T(8,128)S(1)}, u32[]{:S(2)}, u32[]{:S(2)}) collective-permute-start(f32[2,512,128]{2,1,0:T(8,128)S(1)} %get-tuple-element.57), channel_id=1, source_target_pairs={{8,16},{16,8},{9,17},{17,9},{10,18},{18,10},{11,19},{19,11},{12,20... | collective-permute-start | bytes 1572872 | tf_op jit(solution)/shard_map/ppermute | solution.py:25
  46.5 17.0 %collective-permute-start.10 = (f32[2,128,256]{2,1,0:T(8,128)S(1)}, f32[2,128,256]{2,1,0:T(8,128)S(1)}, u32[]{:S(2)}, u32[]{:S(2)}) collective-permute-start(f32[2,128,256]{2,1,0:T(8,128)S(1)} %get-tuple-element.58), channel_id=1, source_target_pairs={{0,1},{1,0},{2,3},{3,2},{4,5},{5,4},{6,7},{7,6},{8,9},{9,8},{10,11... | collective-permute-start | bytes 786440 | tf_op jit(solution)/shard_map/ppermute | solution.py:25
  46.6 18.9 %collective-permute-start.11 = (f32[2,128,256]{2,1,0:T(8,128)S(1)}, f32[2,128,256]{2,1,0:T(8,128)S(1)}, u32[]{:S(2)}, u32[]{:S(2)}) collective-permute-start(f32[2,128,256]{2,1,0:T(8,128)S(1)} %get-tuple-element.59), channel_id=1, source_target_pairs={{1,2},{2,1},{3,4},{4,3},{5,6},{6,5},{9,10},{10,9},{11,12},{12,11},... | collective-permute-start | bytes 786440 | tf_op jit(solution)/shard_map/ppermute | solution.py:25
  48.6 18.5 %collective-permute-start.14 = (f32[2,128,256]{2,1,0:T(8,128)S(1)}, f32[2,128,256]{2,1,0:T(8,128)S(1)}, u32[]{:S(2)}, u32[]{:S(2)}) collective-permute-start(f32[2,128,256]{2,1,0:T(8,128)S(1)} %get-tuple-element.66), channel_id=1, source_target_pairs={{0,1},{1,0},{2,3},{3,2},{4,5},{5,4},{6,7},{7,6},{8,9},{9,8},{10,11... | collective-permute-start | bytes 786440 | tf_op jit(solution)/shard_map/ppermute | solution.py:25
  63.5 9.2 %collective-permute-start.15 = (f32[2,128,256]{2,1,0:T(8,128)S(1)}, f32[2,128,256]{2,1,0:T(8,128)S(1)}, u32[]{:S(2)}, u32[]{:S(2)}) collective-permute-start(f32[2,128,256]{2,1,0:T(8,128)S(1)} %get-tuple-element.67), channel_id=1, source_target_pairs={{1,2},{2,1},{3,4},{4,3},{5,6},{6,5},{9,10},{10,9},{11,12},{12,11},... | collective-permute-start | bytes 786440 | tf_op jit(solution)/shard_map/ppermute | solution.py:25

commit v3 on v2

--- a/solution.py
+++ b/solution.py
@@ -95,8 +95,7 @@
 
 
 def process_slots(
-    first_part, early, plan_ref, scale_ref, probe_ref, tables_ref, amplitudes, extended, total,
-    stages,
+    first_part, plan_ref, scale_ref, probe_ref, tables_ref, amplitudes, extended, total, stages,
 ):
     window = probe_ref.shape[1]
     half = window // 2
@@ -233,7 +232,7 @@
                 else:
                     total[part, tile + 1, at, :] += g[part]
 
-    split = jnp.minimum(plan_ref[0], early)
+    split = plan_ref[0]
     begin, end = (0, split) if first_part else (split, plan_ref[1])
     count = end - begin
 
@@ -318,26 +317,32 @@
     places = subsets * slots
     window = amplitudes.shape[2]
     last_inner = center.shape[1] + HALO - window
-
-    def sort(inner, number, count):
+    near_after = is_after("narrow", NEAR) == 1
+
+    def sort(kind, number, count):
         subset = number // slots
         slot = number - subset * slots
         row = starts_ref[0, 0, subset, 0, slot]
-        inside = (row >= HALO) & (row <= last_inner)
-        mine = (slot < live_ref[0, 0, subset]) & (inside == inner)
+        above, below = row < HALO, row > last_inner
+        near = (near_after & below) | (jnp.logical_not(near_after) & above)
+        inner = (row >= HALO) & (row <= last_inner)
+        wanted = (near, inner, jnp.logical_not(near | inner))[kind]
+        mine = (slot < live_ref[0, 0, subset]) & wanted
 
         @pl.when(mine)
         def _():
             plan[HEAD + count] = number
 
-        if inner:
+        if kind == 0:
             for axis in range(2):
                 plan[HEAD + places + 2 * number + axis] = starts_ref[0, 0, subset, axis, slot]
         return count + mine.astype(jnp.int32)
 
-    inner_count = lax.fori_loop(0, places, functools.partial(sort, True), jnp.int32(0))
-    plan[0] = inner_count
-    plan[1] = lax.fori_loop(0, places, functools.partial(sort, False), inner_count)
+    counts = [jnp.int32(0)]
+    for kind in range(3):
+        counts.append(lax.fori_loop(0, places, functools.partial(sort, kind), counts[-1]))
+    plan[0] = jnp.maximum(counts[1], jnp.minimum(counts[2], EARLY))
+    plan[1] = counts[3]
     total[...] = jnp.zeros_like(total)
     started[0].wait()
     squared = probe[0] * probe[0] + probe[1] * probe[1]
@@ -350,7 +355,7 @@
 
 
 def slots_kernel(
-    n_in, n_out, first_part, early, parts, outputs, plan_ref, scale_ref, probe_ref, tables_ref,
+    n_in, n_out, first_part, parts, outputs, plan_ref, scale_ref, probe_ref, tables_ref,
     amplitudes, *refs,
 ):
     arrived, refs = refs[:n_in], refs[n_in + 2:]
@@ -372,7 +377,7 @@
 
     for ref, here, there in pieces(parts, arrived):
         extended[there] = ref[here]
-    process_slots(first_part, early, plan_ref, scale_ref, probe_ref, tables_ref, amplitudes,
+    process_slots(first_part, plan_ref, scale_ref, probe_ref, tables_ref, amplitudes,
                   extended, total, scratch)
     for ref, here, there in pieces(outputs, outs):
         ref[here] = total[there]
@@ -385,12 +390,12 @@
 MIB = 1024 * 1024
 
 
-def run_slots(first_part, early, common, extended, total, arrived, parts, outputs, out_shapes):
+def run_slots(first_part, common, extended, total, arrived, parts, outputs, out_shapes):
     window = common[2].shape[1]
     f32, bf16 = jnp.float32, jnp.bfloat16
     n = len(common) + len(arrived)
     return pl.pallas_call(
-        functools.partial(slots_kernel, len(arrived), len(out_shapes), first_part, early, parts,
+        functools.partial(slots_kernel, len(arrived), len(out_shapes), first_part, parts,
                           outputs),
         out_shape=[pltpu.VMEM(shape, f32)
                    for shape in [extended.shape, total.shape] + out_shapes],
@@ -424,12 +429,10 @@
                 after, rim[:, :, HALO:], rim[:, :, :HALO])
 
 
-def folded_kernel(near_ends, far_ends, near_rim, far_rim, near, far):
+def folded_kernel(ends, near_rim, far_rim, out):
     left, right = sides("wide", near_rim[...], far_rim[...])
-    for number, (ref, ends) in enumerate(((near, near_ends), (far, far_ends))):
-        rows = slice(number * HALO, (number + 1) * HALO)
-        ref[:, :, :HALO] = ends[:, :, :HALO] + left[:, rows]
-        ref[:, :, HALO:] = ends[:, :, HALO:] + right[:, rows]
+    out[:, :, :HALO] = ends[:, :, :HALO] + left
+    out[:, :, HALO:] = ends[:, :, HALO:] + right
 
 
 def tail_kernel(
@@ -478,7 +481,7 @@
     slots = measured.shape[3]
     tiles = (width + 2 * HALO) // LANES
     whole = (2, tiles, height + 2 * HALO, LANES)
-    wide_rim, side = (2, HALO, width), (2, height, HALO)
+    wide_rim, small_rim, side = (2, HALO, width), (2, HALO, HALO), (2, height, HALO)
     outer, middle = (2, HALO, 2 * HALO), (2, HALO, width - 2 * HALO)
     f32 = jnp.float32
     transmission = pltpu.with_memory_space_constraint(transmission, pltpu.HBM)
@@ -526,7 +529,6 @@
         for x in (jnp.swapaxes(positions, 3, 4), counts, transmission, measured, probe_wave,
                   table)))
     common = (plan, scale, probe, full, amplitudes)
-    near_middle, far_middle = exchange("narrow", near_middle, far_middle)
 
     def small_kernel(kernel, outs, *ins):
         return pl.pallas_call(
@@ -539,31 +541,44 @@
     both = (2, 2 * HALO, HALO)
     near_corner, far_corner = exchange(
         "wide", *small_kernel(ends_kernel, [both] * 2, near_outer, far_outer))
+    near_middle, far_middle = exchange("narrow", near_middle, far_middle)
 
     inner_tiles, ends = tuple(range(2, tiles - 2)), (1, tiles - 2)
     beside = (("wide", NEAR),), (("wide", FAR),)
-    near_row, far_row = ("narrow", NEAR), ("narrow", FAR)
-    extended, total = run_slots(
-        True, EARLY, common, extended, total,
-        (near_columns, far_columns),
-        ((NEAR, 0, HALO, height, beside[NEAR]), (FAR, 0, HALO, height, beside[FAR])), (), [])
-    rows_in = (
-        (0, 0, near_row, HALO, inner_tiles), (1, 0, far_row, HALO, inner_tiles),
-        (2, 0, near_row, HALO, ends), (3, 0, far_row, HALO, ends),
-        *((4 + which, of, row, HALO, beside[which])
-          for which in (NEAR, FAR) for of, row in ((0, near_row), (HALO, far_row))))
-    (extended, total, near_up, far_up, near_ends, far_ends, near_rim, far_rim, near_side,
-     far_side) = run_slots(
-        False, EARLY, common, extended, total,
-        (near_middle, far_middle, near_outer, far_outer, near_corner, far_corner), rows_in,
-        rows_in + ((6, 0, HALO, height, beside[NEAR]), (7, 0, HALO, height, beside[FAR])),
-        [middle, middle, outer, outer, both, both, side, side])
+
+    def rim(which, middle_at, ends_at, corners_at):
+        row = ("narrow", which)
+        return ((middle_at, 0, row, HALO, inner_tiles), (ends_at, 0, row, HALO, ends),
+                *((corners_at + other, which * HALO, row, HALO, beside[other])
+                  for other in (NEAR, FAR)))
+
+    def columns_at(first):
+        return tuple((first + which, 0, HALO, height, beside[which]) for which in (NEAR, FAR))
+
+    def rim_out(which):
+        row = ("narrow", which)
+        return ((0, 0, row, HALO, inner_tiles), (1, 0, row, HALO, ends),
+                (2, 0, row, HALO, beside[NEAR]), (3, 0, row, HALO, beside[FAR]))
+
+    rims = [middle, outer, small_rim, small_rim]
+
+    def folded(rim_ends, near_rim, far_rim):
+        near_rim, far_rim = exchange("wide", near_rim, far_rim)
+        out, = small_kernel(folded_kernel, [outer], rim_ends, near_rim, far_rim)
+        return out
+
+    extended, total, near_up, near_ends, *corners = run_slots(
+        True, common, extended, total,
+        (near_middle, near_outer, near_corner, far_corner, near_columns, far_columns),
+        rim(NEAR, 0, 1, 2) + columns_at(4), rim_out(NEAR), rims)
+    near_ends = folded(near_ends, *corners)
+    extended, total, far_up, far_ends, *corners, near_side, far_side = run_slots(
+        False, common, extended, total,
+        (far_middle, far_outer, near_corner, far_corner), rim(FAR, 0, 1, 2),
+        rim_out(FAR) + columns_at(4), rims + [side, side])
+    far_ends = folded(far_ends, *corners)
     near_up, far_up = exchange("narrow", near_up, far_up)
-    near_rim, far_rim = exchange("wide", near_rim, far_rim)
-
-    near_ends, far_ends = exchange(
-        "narrow", *small_kernel(
-            folded_kernel, [outer] * 2, near_ends, far_ends, near_rim, far_rim))
+    near_ends, far_ends = exchange("narrow", near_ends, far_ends)
     near_side, far_side = exchange("wide", near_side, far_side)
 
     out, head, foot = pl.pallas_call(

time: 74.1 us -> 72.6 us (0.980)
  the two profiles are of different devices: /device:TPU:28 before, /device:TPU:25 now
where the time goes in v3:
time: 72.6 us; the launch traced here: 71.5 us
  starting transfers between devices  31.7 us (44%)
  Pallas kernels  20.5 us (28%)
  waiting for transfers between devices  19.1 us (26%)
    ppermute x18, starting transfers between devices, swapped(): return lax.ppermute(shard, axis, pairs)  31.7 us
    ppermute x18, waiting for transfers between devices, swapped(): return lax.ppermute(shard, axis, pairs)  19.1 us
    pallas_call x2, Pallas kernels, run_slots(): pl.pallas_call(functools.partial(slots_kernel, len(arrived), len(out_shap...  11.4 us
    pallas_call x1, Pallas kernels, update(): pl.pallas_call(setup_kernel, name='setup', out_shape=[pltpu.VMEM(whole, f...  3.67 us
    pallas_call x1, Pallas kernels, update(): pl.pallas_call(tail_kernel, name='tail', out_shape=[jax.ShapeDtypeStruct(...  1.64 us
    pallas_call x1, Pallas kernels, update(): pl.pallas_call(edges_kernel, name='edges', out_shape=[pltpu.VMEM(shape, f...  1.46 us
  transfers between devices with their start and end apart: 18, of which 6 were waited for; matrix products, arithmetic and copies ran while one was open for 0% of the time, Pallas kernels for 18%

profile of v3, /device:TPU:25, one launch (start us, length us, event | category | flops | bytes accessed | tf_op | source)
XLA Modules:
  0.0 71.5 jit_solution(4324142267469496453)
XLA Ops:
  0.0 1.1 %corners.1 = (f32[2,128,256]{2,1,0:T(8,128)S(1)}, f32[2,128,256]{2,1,0:T(8,128)S(1)}) custom-call(f32[2,512,512]{2,1,0:T(8,128)} %center.5), custom_call_target="tpu_custom_call" | custom-call | tf_op jit(solution)/shard_map/corners/pallas_call | solution.py:488
  1.1 3.0 %collective-permute-start.1 = (f32[2,128,256]{2,1,0:T(8,128)S(1)}, f32[2,128,256]{2,1,0:T(8,128)S(1)}, u32[]{:S(2)}, u32[]{:S(2)}) collective-permute-start(f32[2,128,256]{2,1,0:T(8,128)S(1)} %get-tuple-element.43), channel_id=1, source_target_pairs={{1,2},{2,1},{3,4},{4,3},{5,6},{6,5},{9,10},{10,9},{11,12},{12,11},... | collective-permute-start | bytes 786440 | tf_op jit(solution)/shard_map/ppermute | solution.py:25
  4.2 1.5 %edges.1 = (f32[2,512,128]{2,1,0:T(8,128)S(1)}, f32[2,512,128]{2,1,0:T(8,128)S(1)}, f32[2,128,256]{2,1,0:T(8,128)S(1)}, f32[2,128,256]{2,1,0:T(8,128)S(1)}) custom-call(f32[2,512,512]{2,1,0:T(8,128)} %center.5), custom_call_target="tpu_custom_call" | custom-call | tf_op jit(solution)/shard_map/edges/pallas_call | solution.py:501
  5.7 1.0 %collective-permute-start.6 = (f32[2,512,128]{2,1,0:T(8,128)S(1)}, f32[2,512,128]{2,1,0:T(8,128)S(1)}, u32[]{:S(2)}, u32[]{:S(2)}) collective-permute-start(f32[2,512,128]{2,1,0:T(8,128)S(1)} %get-tuple-element.48), channel_id=1, source_target_pairs={{0,8},{8,0},{16,24},{24,16},{1,9},{9,1},{17,25},{25,17},{2,10},{10... | collective-permute-start | bytes 1572872 | tf_op jit(solution)/shard_map/ppermute | solution.py:25
  6.7 3.0 %collective-permute-start.7 = (f32[2,512,128]{2,1,0:T(8,128)S(1)}, f32[2,512,128]{2,1,0:T(8,128)S(1)}, u32[]{:S(2)}, u32[]{:S(2)}) collective-permute-start(f32[2,512,128]{2,1,0:T(8,128)S(1)} %get-tuple-element.49), channel_id=1, source_target_pairs={{8,16},{16,8},{9,17},{17,9},{10,18},{18,10},{11,19},{19,11},{12,20... | collective-permute-start | bytes 1572872 | tf_op jit(solution)/shard_map/ppermute | solution.py:25
  9.8 1.8 %collective-permute-start.5 = (f32[2,128,256]{2,1,0:T(8,128)S(1)}, f32[2,128,256]{2,1,0:T(8,128)S(1)}, u32[]{:S(2)}, u32[]{:S(2)}) collective-permute-start(f32[2,128,256]{2,1,0:T(8,128)S(1)} %get-tuple-element.47), channel_id=1, source_target_pairs={{0,1},{1,0},{2,3},{3,2},{4,5},{5,4},{6,7},{7,6},{8,9},{9,8},{10,11... | collective-permute-start | bytes 786440 | tf_op jit(solution)/shard_map/ppermute | solution.py:25
  11.6 6.2 %collective-permute-done.2.near_outer.refs_1_ = f32[2,128,256]{2,1,0:T(8,128)S(1)} collective-permute-done((f32[2,128,256]{2,1,0:T(8,128)S(1)}, f32[2,128,256]{2,1,0:T(8,128)S(1)}, u32[]{:S(2)}, u32[]{:S(2)}) %collective-permute-start.2) | collective-permute-done | bytes 262176 | tf_op jit(solution)/shard_map/ppermute | solution.py:25
  18.5 3.0 %collective-permute-start.4 = (f32[2,256,128]{2,1,0:T(8,128)S(1)}, f32[2,256,128]{2,1,0:T(8,128)S(1)}, u32[]{:S(2)}, u32[]{:S(2)}) collective-permute-start(f32[2,256,128]{2,1,0:T(8,128)S(1)} %get-tuple-element.46), channel_id=1, source_target_pairs={{8,16},{16,8},{9,17},{17,9},{10,18},{18,10},{11,19},{19,11},{12,20... | collective-permute-start | bytes 786440 | tf_op jit(solution)/shard_map/ppermute | solution.py:25
  21.6 3.7 %setup.1 = (f32[2,6,768,128]{3,2,1,0:T(8,128)S(1)}, f32[2,6,768,128]{3,2,1,0:T(8,128)S(1)}, f32[12,2,256,128]{3,2,1,0:T(8,128)S(1)}, f32[8,128]{1,0:T(8,128)S(1)...) custom-call(s32[1,1,2,2,6]{4,3,2,1,0:T(2,128)} %bitcast.1, s32[1,1,2]{2,1,0:T(1,128)} %live_in.1, ...), custom_call_target="tpu_custom_call" | custom-call | bytes 8388608 | tf_op jit(solution)/shard_map/setup/pallas_call | solution.py:511
  25.2 3.0 %collective-permute-start = (f32[2,128,256]{2,1,0:T(8,128)S(1)}, f32[2,128,256]{2,1,0:T(8,128)S(1)}, u32[]{:S(2)}, u32[]{:S(2)}) collective-permute-start(f32[2,128,256]{2,1,0:T(8,128)S(1)} %get-tuple-element.42), channel_id=1, source_target_pairs={{1,2},{2,1},{3,4},{4,3},{5,6},{6,5},{9,10},{10,9},{11,12},{12,11},... | collective-permute-start | bytes 786440 | tf_op jit(solution)/shard_map/ppermute | solution.py:25
  28.3 6.0 %shard_map.65 = (f32[2,6,768,128]{3,2,1,0:T(8,128)S(1)}, f32[2,6,768,128]{3,2,1,0:T(8,128)S(1)}, f32[2,128,256]{2,1,0:T(8,128)S(1)}, f32[2,128,256]{2,1,0:T(8,12...) custom-call(s32[38]{0:T(128)S(1)} %get-tuple-element.37.plan_ref, ...), custom_call_target="tpu_custom_call", output_to_operand_aliasing={{0}: (11, {}), {1}: (12, {})} | custom-call | flops 3221225472 | bytes 12582912 | tf_op jit(solution)/shard_map/pallas_call | solution.py:397
  34.3 0.9 %collective-permute-done.refs_0_ = f32[2,128,256]{2,1,0:T(8,128)S(1)} collective-permute-done((f32[2,128,256]{2,1,0:T(8,128)S(1)}, f32[2,128,256]{2,1,0:T(8,128)S(1)}, u32[]{:S(2)}, u32[]{:S(2)}) %collective-permute-start) | collective-permute-done | bytes 262176 | tf_op jit(solution)/shard_map/ppermute | solution.py:25
  35.2 5.3 %shard_map.66 = (f32[2,6,768,128]{3,2,1,0:T(8,128)S(1)}, f32[2,6,768,128]{3,2,1,0:T(8,128)S(1)}, f32[2,128,256]{2,1,0:T(8,128)S(1)}, f32[2,128,256]{2,1,0:T(8,12...) custom-call(s32[38]{0:T(128)S(1)} %get-tuple-element.37.plan_ref, ...), custom_call_target="tpu_custom_call", output_to_operand_aliasing={{0}: (9, {}), {1}: (10, {})} | custom-call | flops 3221225472 | bytes 12582912 | tf_op jit(solution)/shard_map/pallas_call | solution.py:397
  41.2 3.4 %collective-permute-start.9 = (f32[2,512,128]{2,1,0:T(8,128)S(1)}, f32[2,512,128]{2,1,0:T(8,128)S(1)}, u32[]{:S(2)}, u32[]{:S(2)}) collective-permute-start(f32[2,512,128]{2,1,0:T(8,128)S(1)} %get-tuple-element.57), channel_id=1, source_target_pairs={{8,16},{16,8},{9,17},{17,9},{10,18},{18,10},{11,19},{19,11},{12,20... | collective-permute-start | bytes 1572872 | tf_op jit(solution)/shard_map/ppermute | solution.py:25
  44.6 1.9 %collective-permute-start.11 = (f32[2,128,256]{2,1,0:T(8,128)S(1)}, f32[2,128,256]{2,1,0:T(8,128)S(1)}, u32[]{:S(2)}, u32[]{:S(2)}) collective-permute-start(f32[2,128,256]{2,1,0:T(8,128)S(1)} %get-tuple-element.59), channel_id=1, source_target_pairs={{1,2},{2,1},{3,4},{4,3},{5,6},{6,5},{9,10},{10,9},{11,12},{12,11},... | collective-permute-start | bytes 786440 | tf_op jit(solution)/shard_map/ppermute | solution.py:25
  46.5 2.1 %collective-permute-start.13 = (f32[2,128,128]{2,1,0:T(8,128)S(1)}, f32[2,128,128]{2,1,0:T(8,128)S(1)}, u32[]{:S(2)}, u32[]{:S(2)}) collective-permute-start(f32[2,128,128]{2,1,0:T(8,128)S(1)} %get-tuple-element.64), channel_id=1, source_target_pairs={{8,16},{16,8},{9,17},{17,9},{10,18},{18,10},{11,19},{19,11},{12,20... | collective-permute-start | bytes 393224 | tf_op jit(solution)/shard_map/ppermute | solution.py:25
  48.7 3.4 %collective-permute-start.16 = (f32[2,128,128]{2,1,0:T(8,128)S(1)}, f32[2,128,128]{2,1,0:T(8,128)S(1)}, u32[]{:S(2)}, u32[]{:S(2)}) collective-permute-start(f32[2,128,128]{2,1,0:T(8,128)S(1)} %get-tuple-element.67), channel_id=1, source_target_pairs={{8,16},{16,8},{9,17},{17,9},{10,18},{18,10},{11,19},{19,11},{12,20... | collective-permute-start | bytes 393224 | tf_op jit(solution)/shard_map/ppermute | solution.py:25
  52.1 1.2 %collective-permute-done.13.far_rim = f32[2,128,128]{2,1,0:T(8,128)S(1)} collective-permute-done((f32[2,128,128]{2,1,0:T(8,128)S(1)}, f32[2,128,128]{2,1,0:T(8,128)S(1)}, u32[]{:S(2)}, u32[]{:S(2)}) %collective-permute-start.13) | collective-permute-done | bytes 131104 | tf_op jit(solution)/shard_map/ppermute | solution.py:25
  53.4 1.9 %collective-permute-done.16.far_rim = f32[2,128,128]{2,1,0:T(8,128)S(1)} collective-permute-done((f32[2,128,128]{2,1,0:T(8,128)S(1)}, f32[2,128,128]{2,1,0:T(8,128)S(1)}, u32[]{:S(2)}, u32[]{:S(2)}) %collective-permute-start.16) | collective-permute-done | bytes 131104 | tf_op jit(solution)/shard_map/ppermute | solution.py:25
  55.3 4.5 %collective-permute-start.17 = (f32[2,128,256]{2,1,0:T(8,128)S(1)}, f32[2,128,256]{2,1,0:T(8,128)S(1)}, u32[]{:S(2)}, u32[]{:S(2)}) collective-permute-start(f32[2,128,256]{2,1,0:T(8,128)S(1)} %shard_map.68), channel_id=1, source_target_pairs={{1,2},{2,1},{3,4},{4,3},{5,6},{6,5},{9,10},{10,9},{11,12},{12,11},... | collective-permute-start | bytes 786440 | tf_op jit(solution)/shard_map/ppermute | solution.py:25
  59.9 7.4 %collective-permute-done.10.near_middle = f32[2,128,256]{2,1,0:T(8,128)S(1)} collective-permute-done((f32[2,128,256]{2,1,0:T(8,128)S(1)}, f32[2,128,256]{2,1,0:T(8,128)S(1)}, u32[]{:S(2)}, u32[]{:S(2)}) %collective-permute-start.10) | collective-permute-done | bytes 262176 | tf_op jit(solution)/shard_map/ppermute | solution.py:25
  67.3 1.6 %tail.1 = (f32[2,512,512]{2,1,0:T(8,128)}, f32[2,128,512]{2,1,0:T(8,128)S(1)}, f32[2,128,512]{2,1,0:T(8,128)S(1)}) custom-call(f32[2,6,768,128]{3,2,1,0:T(8,128)S(1)} %get-tuple-element.54.extended, f32[2,6,768,128]{3,2,1,0:T(8,128)S(1)} %get-tuple-element.55.total, f32[2,512,128]{2,1,0:T(8,128)S(1)} %collective-permute-done.8.near_side, ...), custom_call_target="tpu_custom_call" | custom-call | tf_op jit(solution)/shard_map/tail/pallas_call | solution.py:584
  69.0 1.5 %collective-permute-done.14.near_outer = f32[2,128,256]{2,1,0:T(8,128)S(1)} collective-permute-done((f32[2,128,256]{2,1,0:T(8,128)S(1)}, f32[2,128,256]{2,1,0:T(8,128)S(1)}, u32[]{:S(2)}, u32[]{:S(2)}) %collective-permute-start.14) | collective-permute-done | bytes 262176 | tf_op jit(solution)/shard_map/ppermute | solution.py:25
  70.4 1.1 %rims.1 = f32[2,512,512]{2,1,0:T(8,128)} custom-call(f32[2,128,512]{2,1,0:T(8,128)S(1)} %get-tuple-element.60.head, f32[2,128,512]{2,1,0:T(8,128)S(1)} %get-tuple-element.61.foot, f32[2,128,256]{2,1,0:T(8,128)S(1)} %collective-permute-done.14.near_outer, f32[2,128,256]{2,1,0:T(8,128)S(1)} %collective-permute-done.17.far_outer, ...), custom_call_target="tpu_custom_call", output_to_operand_aliasing={{}: (4, {})} | custom-call | tf_op jit(solution)/shard_map/rims/pallas_call | solution.py:592
  (22 shorter events, 1.6 us)
Async XLA Ops:
  1.1 10.4 %collective-permute-start.1 = (f32[2,128,256]{2,1,0:T(8,128)S(1)}, f32[2,128,256]{2,1,0:T(8,128)S(1)}, u32[]{:S(2)}, u32[]{:S(2)}) collective-permute-start(f32[2,128,256]{2,1,0:T(8,128)S(1)} %get-tuple-element.43), channel_id=1, source_target_pairs={{1,2},{2,1},{3,4},{4,3},{5,6},{6,5},{9,10},{10,9},{11,12},{12,11},... | collective-permute-start | bytes 786440 | tf_op jit(solution)/shard_map/ppermute | solution.py:25
  4.2 13.6 %collective-permute-start.2 = (f32[2,128,256]{2,1,0:T(8,128)S(1)}, f32[2,128,256]{2,1,0:T(8,128)S(1)}, u32[]{:S(2)}, u32[]{:S(2)}) collective-permute-start(f32[2,128,256]{2,1,0:T(8,128)S(1)} %get-tuple-element.44), channel_id=1, source_target_pairs={{0,1},{1,0},{2,3},{3,2},{4,5},{5,4},{6,7},{7,6},{8,9},{9,8},{10,11... | collective-permute-start | bytes 786440 | tf_op jit(solution)/shard_map/ppermute | solution.py:25
  5.7 22.5 %collective-permute-start.6 = (f32[2,512,128]{2,1,0:T(8,128)S(1)}, f32[2,512,128]{2,1,0:T(8,128)S(1)}, u32[]{:S(2)}, u32[]{:S(2)}) collective-permute-start(f32[2,512,128]{2,1,0:T(8,128)S(1)} %get-tuple-element.48), channel_id=1, source_target_pairs={{0,8},{8,0},{16,24},{24,16},{1,9},{9,1},{17,25},{25,17},{2,10},{10... | collective-permute-start | bytes 1572872 | tf_op jit(solution)/shard_map/ppermute | solution.py:25
  6.7 21.5 %collective-permute-start.7 = (f32[2,512,128]{2,1,0:T(8,128)S(1)}, f32[2,512,128]{2,1,0:T(8,128)S(1)}, u32[]{:S(2)}, u32[]{:S(2)}) collective-permute-start(f32[2,512,128]{2,1,0:T(8,128)S(1)} %get-tuple-element.49), channel_id=1, source_target_pairs={{8,16},{16,8},{9,17},{17,9},{10,18},{18,10},{11,19},{19,11},{12,20... | collective-permute-start | bytes 1572872 | tf_op jit(solution)/shard_map/ppermute | solution.py:25
  9.8 15.5 %collective-permute-start.5 = (f32[2,128,256]{2,1,0:T(8,128)S(1)}, f32[2,128,256]{2,1,0:T(8,128)S(1)}, u32[]{:S(2)}, u32[]{:S(2)}) collective-permute-start(f32[2,128,256]{2,1,0:T(8,128)S(1)} %get-tuple-element.47), channel_id=1, source_target_pairs={{0,1},{1,0},{2,3},{3,2},{4,5},{5,4},{6,7},{7,6},{8,9},{9,8},{10,11... | collective-permute-start | bytes 786440 | tf_op jit(solution)/shard_map/ppermute | solution.py:25
  17.8 10.4 %collective-permute-start.3 = (f32[2,256,128]{2,1,0:T(8,128)S(1)}, f32[2,256,128]{2,1,0:T(8,128)S(1)}, u32[]{:S(2)}, u32[]{:S(2)}) collective-permute-start(f32[2,256,128]{2,1,0:T(8,128)S(1)} %get-tuple-element.45), channel_id=1, source_target_pairs={{0,8},{8,0},{16,24},{24,16},{1,9},{9,1},{17,25},{25,17},{2,10},{10... | collective-permute-start | bytes 786440 | tf_op jit(solution)/shard_map/ppermute | solution.py:25
  18.5 9.7 %collective-permute-start.4 = (f32[2,256,128]{2,1,0:T(8,128)S(1)}, f32[2,256,128]{2,1,0:T(8,128)S(1)}, u32[]{:S(2)}, u32[]{:S(2)}) collective-permute-start(f32[2,256,128]{2,1,0:T(8,128)S(1)} %get-tuple-element.46), channel_id=1, source_target_pairs={{8,16},{16,8},{9,17},{17,9},{10,18},{18,10},{11,19},{19,11},{12,20... | collective-permute-start | bytes 786440 | tf_op jit(solution)/shard_map/ppermute | solution.py:25
  25.2 9.9 %collective-permute-start = (f32[2,128,256]{2,1,0:T(8,128)S(1)}, f32[2,128,256]{2,1,0:T(8,128)S(1)}, u32[]{:S(2)}, u32[]{:S(2)}) collective-permute-start(f32[2,128,256]{2,1,0:T(8,128)S(1)} %get-tuple-element.42), channel_id=1, source_target_pairs={{1,2},{2,1},{3,4},{4,3},{5,6},{6,5},{9,10},{10,9},{11,12},{12,11},... | collective-permute-start | bytes 786440 | tf_op jit(solution)/shard_map/ppermute | solution.py:25
  40.5 6.0 %collective-permute-start.15 = (f32[2,128,128]{2,1,0:T(8,128)S(1)}, f32[2,128,128]{2,1,0:T(8,128)S(1)}, u32[]{:S(2)}, u32[]{:S(2)}) collective-permute-start(f32[2,128,128]{2,1,0:T(8,128)S(1)} %get-tuple-element.66), channel_id=1, source_target_pairs={{0,8},{8,0},{16,24},{24,16},{1,9},{9,1},{17,25},{25,17},{2,10},{10... | collective-permute-start | bytes 393224 | tf_op jit(solution)/shard_map/ppermute | solution.py:25
  40.6 8.1 %collective-permute-start.12 = (f32[2,128,128]{2,1,0:T(8,128)S(1)}, f32[2,128,128]{2,1,0:T(8,128)S(1)}, u32[]{:S(2)}, u32[]{:S(2)}) collective-permute-start(f32[2,128,128]{2,1,0:T(8,128)S(1)} %get-tuple-element.63), channel_id=1, source_target_pairs={{0,8},{8,0},{16,24},{24,16},{1,9},{9,1},{17,25},{25,17},{2,10},{10... | collective-permute-start | bytes 393224 | tf_op jit(solution)/shard_map/ppermute | solution.py:25
  41.1 26.2 %collective-permute-start.8 = (f32[2,512,128]{2,1,0:T(8,128)S(1)}, f32[2,512,128]{2,1,0:T(8,128)S(1)}, u32[]{:S(2)}, u32[]{:S(2)}) collective-permute-start(f32[2,512,128]{2,1,0:T(8,128)S(1)} %get-tuple-element.56), channel_id=1, source_target_pairs={{0,8},{8,0},{16,24},{24,16},{1,9},{9,1},{17,25},{25,17},{2,10},{10... | collective-permute-start | bytes 1572872 | tf_op jit(solution)/shard_map/ppermute | solution.py:25
  41.2 26.1 %collective-permute-start.9 = (f32[2,512,128]{2,1,0:T(8,128)S(1)}, f32[2,512,128]{2,1,0:T(8,128)S(1)}, u32[]{:S(2)}, u32[]{:S(2)}) collective-permute-start(f32[2,512,128]{2,1,0:T(8,128)S(1)} %get-tuple-element.57), channel_id=1, source_target_pairs={{8,16},{16,8},{9,17},{17,9},{10,18},{18,10},{11,19},{19,11},{12,20... | collective-permute-start | bytes 1572872 | tf_op jit(solution)/shard_map/ppermute | solution.py:25
  44.6 10.7 %collective-permute-start.11 = (f32[2,128,256]{2,1,0:T(8,128)S(1)}, f32[2,128,256]{2,1,0:T(8,128)S(1)}, u32[]{:S(2)}, u32[]{:S(2)}) collective-permute-start(f32[2,128,256]{2,1,0:T(8,128)S(1)} %get-tuple-element.59), channel_id=1, source_target_pairs={{1,2},{2,1},{3,4},{4,3},{5,6},{6,5},{9,10},{10,9},{11,12},{12,11},... | collective-permute-start | bytes 786440 | tf_op jit(solution)/shard_map/ppermute | solution.py:25
  46.5 6.8 %collective-permute-start.13 = (f32[2,128,128]{2,1,0:T(8,128)S(1)}, f32[2,128,128]{2,1,0:T(8,128)S(1)}, u32[]{:S(2)}, u32[]{:S(2)}) collective-permute-start(f32[2,128,128]{2,1,0:T(8,128)S(1)} %get-tuple-element.64), channel_id=1, source_target_pairs={{8,16},{16,8},{9,17},{17,9},{10,18},{18,10},{11,19},{19,11},{12,20... | collective-permute-start | bytes 393224 | tf_op jit(solution)/shard_map/ppermute | solution.py:25
  48.7 6.6 %collective-permute-start.16 = (f32[2,128,128]{2,1,0:T(8,128)S(1)}, f32[2,128,128]{2,1,0:T(8,128)S(1)}, u32[]{:S(2)}, u32[]{:S(2)}) collective-permute-start(f32[2,128,128]{2,1,0:T(8,128)S(1)} %get-tuple-element.67), channel_id=1, source_target_pairs={{8,16},{16,8},{9,17},{17,9},{10,18},{18,10},{11,19},{19,11},{12,20... | collective-permute-start | bytes 393224 | tf_op jit(solution)/shard_map/ppermute | solution.py:25
  53.4 13.9 %collective-permute-start.10 = (f32[2,128,256]{2,1,0:T(8,128)S(1)}, f32[2,128,256]{2,1,0:T(8,128)S(1)}, u32[]{:S(2)}, u32[]{:S(2)}) collective-permute-start(f32[2,128,256]{2,1,0:T(8,128)S(1)} %get-tuple-element.58), channel_id=1, source_target_pairs={{0,1},{1,0},{2,3},{3,2},{4,5},{5,4},{6,7},{7,6},{8,9},{9,8},{10,11... | collective-permute-start | bytes 786440 | tf_op jit(solution)/shard_map/ppermute | solution.py:25
  55.3 15.2 %collective-permute-start.14 = (f32[2,128,256]{2,1,0:T(8,128)S(1)}, f32[2,128,256]{2,1,0:T(8,128)S(1)}, u32[]{:S(2)}, u32[]{:S(2)}) collective-permute-start(f32[2,128,256]{2,1,0:T(8,128)S(1)} %shard_map.67), channel_id=1, source_target_pairs={{0,1},{1,0},{2,3},{3,2},{4,5},{5,4},{6,7},{7,6},{8,9},{9,8},{10,11... | collective-permute-start | bytes 786440 | tf_op jit(solution)/shard_map/ppermute | solution.py:25
  55.3 15.1 %collective-permute-start.17 = (f32[2,128,256]{2,1,0:T(8,128)S(1)}, f32[2,128,256]{2,1,0:T(8,128)S(1)}, u32[]{:S(2)}, u32[]{:S(2)}) collective-permute-start(f32[2,128,256]{2,1,0:T(8,128)S(1)} %shard_map.68), channel_id=1, source_target_pairs={{1,2},{2,1},{3,4},{4,3},{5,6},{6,5},{9,10},{10,9},{11,12},{12,11},... | collective-permute-start | bytes 786440 | tf_op jit(solution)/shard_map/ppermute | solution.py:25
